TPU v7x, 32 devices: a whole 2x2x4 slice. The times are simulated.
32 devices in a mesh: seq: 4 (over z), dp: 8 (over y, x, core).
Axes of the slice: x: 2, y: 2, z: 4, core: 2. Of those that a mesh axis runs over, the one named last changes fastest.
Arguments:
- stream: float32 [8, 512, 1152], P('dp', 'seq'), may hold values from -50 to 50
- stream_grad: float32 [8, 512, 1152], P('dp', 'seq'), may hold values from -6 to 6
- lengths: int32 [8, 4], P('dp'), may hold values from 1 to 384, 512 in all within a row
- w_qkv: bfloat16 [1152, 1536], P(('seq', 'dp')), may hold values from -0.1875 to 0.1875
- w_out: bfloat16 [1024, 1152], P(('seq', 'dp')), may hold values from -0.1875 to 0.1875
- w_gate: bfloat16 [6912, 1152], P(('seq', 'dp')), may hold values from -0.1875 to 0.1875
- w_up: bfloat16 [6912, 1152], P(('seq', 'dp')), may hold values from -0.1875 to 0.1875
- w_down: bfloat16 [6912, 1152], P(('seq', 'dp')), may hold values from -0.078125 to 0.078125
- g_attn_in: float32 [1152], replicated, may hold values from 0.25 to 1.75
- g_query: float32 [256], replicated, may hold values from 0.25 to 1.75
- g_key: float32 [256], replicated, may hold values from 0.25 to 1.75
- g_attn_out: float32 [1152], replicated, may hold values from 0.25 to 1.75
- g_ffn_in: float32 [1152], replicated, may hold values from 0.25 to 1.75
- g_ffn_out: float32 [1152], replicated, may hold values from 0.25 to 1.75
Outputs:
- result: float32 [8, 512, 1152], P('dp', 'seq')
- input_grad: float32 [8, 512, 1152], P('dp', 'seq')
- grad_w_qkv: float32 [1152, 1536], P(('seq', 'dp'))
- grad_w_out: float32 [1024, 1152], P(('seq', 'dp'))
- grad_w_gate: float32 [6912, 1152], P(('seq', 'dp'))
- grad_w_up: float32 [6912, 1152], P(('seq', 'dp'))
- grad_w_down: float32 [6912, 1152], P(('seq', 'dp'))
- grad_g_attn_in: float32 [1152], P(('seq', 'dp'))
- grad_g_query: float32 [256], P(('seq', 'dp'))
- grad_g_key: float32 [256], P(('seq', 'dp'))
- grad_g_attn_out: float32 [1152], P(('seq', 'dp'))
- grad_g_ffn_in: float32 [1152], P(('seq', 'dp'))
- grad_g_ffn_out: float32 [1152], P(('seq', 'dp'))
Inputs may be any that keep to these rules, and one draw needn't show every extreme that they name: Each row lists the lengths of the 4 sequences packed in order into one group; they sum to 512.
All inputs are finite; a program needn't handle non-finite values.
Results may differ from a plain program's by a relative error of at most 0.015.
Values may be sent and summed in bfloat16 or wider, within the bound.
A program may use at most 128 MiB of HBM per device.

v0:
```python
import math

import jax
import jax.numpy as jnp
from jax import lax
from jax.sharding import PartitionSpec as P

HEADS = 4
HEAD_DIM = 256
WINDOW = 512


EPSILON = 1e-06
GELU_SLOPE = math.sqrt(2.0 / math.pi)
GELU_CUBIC = 0.044715


def bits_of(count):
    bits = []
    bit = 1
    while bit < count:
        bits.append(bit)
        bit *= 2
    return bits


def swapped(value, axis, bit):
    length = lax.axis_size(axis)
    return lax.ppermute(value, axis, [(i, i ^ bit) for i in range(length)])


def mine_first(value, axis, bit, at):
    return jnp.concatenate([value, swapped(value, axis, bit)], axis=at)


def keep_half(value, axis, bit, at):
    own = lax.slice_in_dim(value, 0, 1, axis=at)
    other = lax.slice_in_dim(value, 1, 2, axis=at).astype(jnp.bfloat16)
    return own.astype(jnp.float32) + swapped(other, axis, bit).astype(jnp.float32)


def gather_xor(value, stages):
    value = value.reshape((1,) * len(stages) + value.shape)
    for axis, bit, at in stages:
        value = mine_first(value, axis, bit, at)
    return value


def scatter_xor(value, stages):
    for axis, bit, at in stages:
        value = keep_half(value, axis, bit, at)
    return value.reshape(value.shape[len(stages) :])


def one_hot_order(origin, count):
    return (jnp.arange(count, dtype=jnp.int32)[:, None] == origin[None, :]).astype(jnp.bfloat16)


def in_order(value, order):
    return lax.dot_general(
        value.astype(jnp.float32),
        order.astype(jnp.float32),
        (((1,), (1,)), ((), ())),
        precision=lax.Precision.HIGHEST,
        preferred_element_type=jnp.float32,
    )


def inv_root(vector):
    return lax.rsqrt(jnp.mean(vector * vector, axis=-1, keepdims=True) + EPSILON)


def norm_back(grad, unit_part, root_part, gain):
    scaled = grad * gain
    return root_part * (scaled - unit_part * jnp.mean(scaled * unit_part, axis=-1, keepdims=True))


def gelu_pair(gate):
    inner = jnp.tanh(GELU_SLOPE * (gate + GELU_CUBIC * gate * gate * gate))
    gelu_value = 0.5 * gate * (1.0 + inner)
    gelu_slope = 0.5 * (1.0 + inner) + 0.5 * gate * (1.0 - inner * inner) * GELU_SLOPE * (
        1.0 + 3.0 * GELU_CUBIC * gate * gate
    )
    return (gelu_value, gelu_slope)


def turn_half(vector):
    half = vector.shape[-1] // 2
    return jnp.concatenate([-vector[..., half:], vector[..., :half]], axis=-1)


def seq_begin(index, starts):
    return jnp.max(jnp.where(starts[None, :] <= index[:, None], starts[None, :], 0), axis=1)


def rope_tables(position, head):
    freq = jnp.exp(-math.log(10000.0) * jnp.arange(head // 2, dtype=jnp.float32) * (2.0 / head))
    angle = position[:, None] * freq[None, :]
    angle = jnp.concatenate([angle, angle], axis=1)
    return (jnp.cos(angle), jnp.sin(angle))


def dot32(left, right):
    return jnp.dot(left, right, preferred_element_type=jnp.float32)


def contract_rows(left, right):
    return lax.dot_general(
        left, right, (((0,), (0,)), ((), ())), preferred_element_type=jnp.float32
    )


def contract_cols(left, right):
    return lax.dot_general(
        left, right, (((1,), (1,)), ((), ())), preferred_element_type=jnp.float32
    )


def ffn_forward_fold(tokens_b, pieces):
    gate_rows, up_rows, down_rows = pieces
    gate_part = contract_cols(tokens_b, gate_rows)
    up_part = contract_cols(tokens_b, up_rows)
    gelu_value, gelu_slope = gelu_pair(gate_part)
    hidden = (gelu_value * up_part).astype(jnp.bfloat16)
    out_total = dot32(hidden, down_rows)
    return (out_total, gate_part, up_part)


def ffn_backward_fold(grad_b, gate_all, up_all, pieces):
    gate_rows, up_rows, down_rows = pieces
    hidden_grad = contract_cols(grad_b, down_rows)
    gelu_value, gelu_slope = gelu_pair(gate_all)
    dgate_b = (hidden_grad * up_all * gelu_slope).astype(jnp.bfloat16)
    dup_b = (hidden_grad * gelu_value).astype(jnp.bfloat16)
    in_total = dot32(dgate_b, gate_rows) + dot32(dup_b, up_rows)
    return (in_total, dgate_b, dup_b)


def ffn_weight_terms(tokens_b, grad_b, gate_all, up_all, dgate_all, dup_all):
    gelu_value, gelu_slope = gelu_pair(gate_all)
    hidden = (gelu_value * up_all).astype(jnp.bfloat16)
    return (
        contract_rows(dgate_all, tokens_b),
        contract_rows(dup_all, tokens_b),
        contract_rows(hidden, grad_b),
    )


def local(
    stream,
    stream_grad,
    lengths,
    w_qkv,
    w_out,
    w_gate,
    w_up,
    w_down,
    g_attn_in,
    g_query,
    g_key,
    g_attn_out,
    g_ffn_in,
    g_ffn_out,
):
    rows_in = stream[0]
    rows_grad = stream_grad[0]
    lens = lengths[0]
    rows = rows_in.shape[0]
    width = rows_in.shape[1]
    qwidth = HEADS * HEAD_DIM
    seq_count = lax.axis_size("seq")
    chip_bits = [2 * bit for bit in bits_of(lax.axis_size("dp") // 2)]
    seq_bits = bits_of(seq_count)
    nseq, nchip = len(seq_bits), len(chip_bits)
    seq_stages = [("seq", bit, nseq - 1 - k) for k, bit in enumerate(seq_bits)][::-1]
    chip_stages = [("dp", bit, nseq + nchip - 1 - k) for k, bit in enumerate(chip_bits)]
    core_stage = [("dp", 1, nseq + nchip)]
    all_up = seq_stages + chip_stages + core_stage
    all_down = seq_stages + chip_stages[::-1] + core_stage
    dp_count = lax.axis_size("dp")
    chips = dp_count // 2
    plane_up = [("dp", bit, nchip - 1 - k) for k, bit in enumerate(chip_bits)]
    plane_down = plane_up[::-1]
    cut = (width // 256) * 128 + (128 if width % 256 else 0)
    kv_stages = seq_stages
    keys = seq_count * rows
    scale = 1.0 / math.sqrt(HEAD_DIM)
    block_id = lax.axis_index("seq")
    dp_id = lax.axis_index("dp")
    seq_off = jnp.arange(seq_count, dtype=jnp.int32)
    chip_off = jnp.arange(chips, dtype=jnp.int32)
    core_off = jnp.arange(2, dtype=jnp.int32)
    qkv_own = w_qkv.shape[0]
    qkv_pad = (qkv_own + 8) // 8 * 8
    out_own = w_out.shape[0]
    ffn_own = w_gate.shape[0]
    half = w_qkv.shape[1] // 2
    qkv_dev = (
        (block_id ^ seq_off)[:, None, None] * dp_count
        + ((dp_id // 2) ^ chip_off)[None, :, None] * 2
        + ((dp_id % 2) ^ core_off)[None, None, :]
    ).reshape(-1, 1)
    lane = jnp.arange(qkv_pad, dtype=jnp.int32)[None, :]
    qkv_origin = jnp.where(lane < qkv_own, qkv_dev * qkv_own + lane, -1).reshape(-1)
    out_dev = qkv_dev
    out_origin = (out_dev * out_own + jnp.arange(out_own, dtype=jnp.int32)[None, :]).reshape(-1)
    qkv_order = one_hot_order(qkv_origin, width)
    out_order = one_hot_order(out_origin, qwidth)
    w_qkv_pad = jnp.pad(w_qkv, ((0, qkv_pad - qkv_own), (0, 0)))
    qkv_full = jnp.concatenate(
        [
            gather_xor(w_qkv_pad[:, :half], all_up),
            gather_xor(w_qkv_pad[:, half:], all_down),
        ],
        axis=-1,
    ).reshape(-1, 2 * half)
    out_full = gather_xor(w_out, all_down).reshape(-1, width)
    line_rows = lax.all_gather(
        jnp.concatenate([w_gate, w_up, w_down], axis=0),
        "seq",
        axis=0,
    )
    gate_full, up_full, down_full = (
        line_rows[:, i * ffn_own : (i + 1) * ffn_own].reshape(-1, width) for i in range(3)
    )
    starts = jnp.cumsum(lens) - lens
    own_index = block_id * rows + jnp.arange(rows, dtype=jnp.int32)
    key_index = (
        (block_id ^ jnp.arange(seq_count, dtype=jnp.int32))[:, None] * rows
        + jnp.arange(rows, dtype=jnp.int32)[None, :]
    ).reshape(keys)
    own_begin = seq_begin(own_index, starts)
    key_begin = seq_begin(key_index, starts)
    mask = (
        (key_begin[None, :] == own_begin[:, None])
        & (key_index[None, :] <= own_index[:, None])
        & (own_index[:, None] - key_index[None, :] < WINDOW)
    )
    full_mask = mask[:, None, :]
    cos_t, sin_t = rope_tables((own_index - own_begin).astype(jnp.float32), HEAD_DIM)
    root_attn = inv_root(rows_in)
    unit_attn = rows_in * root_attn
    attn_input = (unit_attn * g_attn_in).astype(jnp.bfloat16)
    attn_slots = dot32(attn_input, qkv_order).astype(jnp.bfloat16)
    projected = dot32(attn_slots, qkv_full)
    query = projected[:, :qwidth].reshape(rows, HEADS, HEAD_DIM)
    key_raw = projected[:, qwidth : qwidth + HEAD_DIM]
    value_raw = projected[:, qwidth + HEAD_DIM :]
    root_query = inv_root(query)
    unit_query = query * root_query
    query_norm = unit_query * g_query
    root_key = inv_root(key_raw)
    unit_key = key_raw * root_key
    key_norm = unit_key * g_key
    query_rot = query_norm * cos_t[:, None, :] + turn_half(query_norm) * sin_t[:, None, :]
    key_rot = key_norm * cos_t + turn_half(key_norm) * sin_t
    query_b = query_rot.astype(jnp.bfloat16)
    kv_own = jnp.concatenate([key_rot.astype(jnp.bfloat16), value_raw.astype(jnp.bfloat16)], axis=1)
    kv_all = gather_xor(kv_own, kv_stages).reshape(keys, 2 * HEAD_DIM)
    keys_b = kv_all[:, :HEAD_DIM]
    values_b = kv_all[:, HEAD_DIM:]
    scores = jnp.einsum("rhd,kd->rhk", query_b, keys_b, preferred_element_type=jnp.float32) * scale
    logsum = jnp.log(jnp.sum(jnp.where(full_mask, jnp.exp(scores), 0.0), axis=-1))
    probs = jnp.where(full_mask, jnp.exp(scores - logsum[..., None]), 0.0)
    probs_b = probs.astype(jnp.bfloat16)
    mixed = jnp.einsum("rhk,kd->rhd", probs_b, values_b, preferred_element_type=jnp.float32)
    mixed_b = mixed.reshape(rows, qwidth).astype(jnp.bfloat16)
    mixed_slots = dot32(mixed_b, out_order).astype(jnp.bfloat16)
    attn_out = dot32(mixed_slots, out_full)
    root_post = inv_root(attn_out)
    unit_post = attn_out * root_post
    hidden_in = rows_in + unit_post * g_attn_out
    root_ffn = inv_root(hidden_in)
    unit_ffn = hidden_in * root_ffn
    ffn_input = (unit_ffn * g_ffn_in).astype(jnp.bfloat16)

    def gather_tokens(value):
        both = jnp.concatenate(
            [gather_xor(value[:, :cut], plane_up), gather_xor(value[:, cut:], plane_down)], axis=-1
        )
        return mine_first(both[None], "dp", 1, 0).reshape(-1, width)

    def scatter_tokens(value):
        value = keep_half(value.reshape((2,) * (1 + nchip) + (rows, width)), "dp", 1, 0)[0]
        return jnp.concatenate(
            [
                scatter_xor(value[..., :cut], plane_down),
                scatter_xor(value[..., cut:], plane_up),
            ],
            axis=-1,
        )

    tokens_b = gather_tokens(ffn_input)
    out_part, gate_all, up_all = ffn_forward_fold(tokens_b, (gate_full, up_full, down_full))
    ffn_out = scatter_tokens(out_part)
    root_out = inv_root(ffn_out)
    unit_out = ffn_out * root_out
    result = hidden_in + unit_out * g_ffn_out
    grad_g_ffn_out = jnp.sum(rows_grad * unit_out, axis=0)
    ffn_grad_b = norm_back(rows_grad, unit_out, root_out, g_ffn_out).astype(jnp.bfloat16)
    grads_b = gather_tokens(ffn_grad_b)
    in_part, dgate_all, dup_all = ffn_backward_fold(
        grads_b, gate_all, up_all, (gate_full, up_full, down_full)
    )
    ffn_in_grad = scatter_tokens(in_part)
    terms = ffn_weight_terms(tokens_b, grads_b, gate_all, up_all, dgate_all, dup_all)
    ffn_in_grad, term_rows = lax.optimization_barrier(
        (
            ffn_in_grad,
            jnp.concatenate(
                [term.astype(jnp.bfloat16).reshape(seq_count, ffn_own, width) for term in terms],
                axis=1,
            ),
        )
    )
    ffn_terms = lax.psum_scatter(term_rows, "seq", scatter_dimension=0).astype(jnp.float32)
    ffn_terms = ffn_terms.reshape(3, ffn_own, width)
    grad_w_gate, grad_w_up, grad_w_down = ffn_terms[0], ffn_terms[1], ffn_terms[2]
    grad_g_ffn_in = jnp.sum(ffn_in_grad * unit_ffn, axis=0)
    hidden_grad_in = rows_grad + norm_back(ffn_in_grad, unit_ffn, root_ffn, g_ffn_in)
    grad_g_attn_out = jnp.sum(hidden_grad_in * unit_post, axis=0)
    attn_grad_b = norm_back(hidden_grad_in, unit_post, root_post, g_attn_out).astype(jnp.bfloat16)
    mixed_grad_slots = contract_cols(attn_grad_b, out_full).astype(jnp.bfloat16)
    mixed_grad_b = contract_cols(mixed_grad_slots, out_order).astype(jnp.bfloat16)
    spread = (2,) * (nseq + nchip + 1)
    out_term = contract_rows(mixed_slots, attn_grad_b).reshape(spread + w_out.shape)
    owned_out = scatter_xor(out_term, all_down[::-1])
    mixed_grad3 = mixed_grad_b.reshape(rows, HEADS, HEAD_DIM)
    delta = jnp.sum(
        mixed_grad3.astype(jnp.float32)
        * mixed_b.reshape(rows, HEADS, HEAD_DIM).astype(jnp.float32),
        axis=-1,
    )
    scores_again = (
        jnp.einsum("rhd,kd->rhk", query_b, keys_b, preferred_element_type=jnp.float32) * scale
    )
    probs_again = jnp.where(full_mask, jnp.exp(scores_again - logsum[..., None]), 0.0)
    probs_again_b = probs_again.astype(jnp.bfloat16)
    value_grad_all = jnp.einsum(
        "rhk,rhd->kd", probs_again_b, mixed_grad3, preferred_element_type=jnp.float32
    )
    prob_grad = jnp.einsum("rhd,kd->rhk", mixed_grad3, values_b, preferred_element_type=jnp.float32)
    score_grad_b = (probs_again * (prob_grad - delta[..., None])).astype(jnp.bfloat16)
    query_rot_grad = (
        jnp.einsum("rhk,kd->rhd", score_grad_b, keys_b, preferred_element_type=jnp.float32) * scale
    )
    key_grad_all = (
        jnp.einsum("rhk,rhd->kd", score_grad_b, query_b, preferred_element_type=jnp.float32) * scale
    )
    kv_grad_all = jnp.concatenate([key_grad_all, value_grad_all], axis=1)
    kv_grad = scatter_xor(
        kv_grad_all.reshape((2,) * nseq + (rows, 2 * HEAD_DIM)), kv_stages[::-1]
    )
    kv_grad, owned_out = lax.optimization_barrier((kv_grad, owned_out))
    key_rot_grad = kv_grad[:, :HEAD_DIM]
    value_grad = kv_grad[:, HEAD_DIM:]
    query_norm_grad = query_rot_grad * cos_t[:, None, :] - turn_half(
        query_rot_grad * sin_t[:, None, :]
    )
    key_norm_grad = key_rot_grad * cos_t - turn_half(key_rot_grad * sin_t)
    grad_g_query = jnp.sum(query_norm_grad * unit_query, axis=(0, 1))
    grad_g_key = jnp.sum(key_norm_grad * unit_key, axis=0)
    query_grad = norm_back(query_norm_grad, unit_query, root_query, g_query)
    key_grad = norm_back(key_norm_grad, unit_key, root_key, g_key)
    qkv_grad_b = jnp.concatenate(
        [query_grad.reshape(rows, qwidth), key_grad, value_grad], axis=1
    ).astype(jnp.bfloat16)
    attn_in_grad = in_order(contract_cols(qkv_grad_b, qkv_full), qkv_order)
    grad_g_attn_in = jnp.sum(attn_in_grad * unit_attn, axis=0)
    input_grad = hidden_grad_in + norm_back(attn_in_grad, unit_attn, root_attn, g_attn_in)
    spread = (2,) * (nseq + nchip + 1)
    count = seq_count * lax.axis_size("dp")
    gains = [grad_g_attn_in, grad_g_attn_out, grad_g_ffn_in, grad_g_ffn_out, grad_g_query, grad_g_key]
    gain_terms = jnp.concatenate([g.reshape(count, -1) for g in gains], axis=1)
    qkv_term = contract_rows(attn_slots, qkv_grad_b).reshape(spread + (qkv_pad, 2 * half))
    gain_slots = jnp.take(gain_terms, qkv_dev.reshape(-1), axis=0)
    left_term = qkv_term[..., :half].at[..., qkv_own, : gain_slots.shape[1]].set(
        gain_slots.reshape(spread + (-1,))
    )
    left_owned = scatter_xor(left_term, all_up[::-1])
    right_owned = scatter_xor(qkv_term[..., half:], all_down[::-1])
    owned_qkv = jnp.concatenate([left_owned, right_owned], axis=-1)[:qkv_own]
    owned = left_owned[qkv_own]
    own_width, own_head = width // count, HEAD_DIM // count
    owned_gains = [owned[i * own_width : (i + 1) * own_width] for i in range(4)]
    owned_heads = [
        owned[4 * own_width + i * own_head : 4 * own_width + (i + 1) * own_head] for i in range(2)
    ]
    return (
        result[None],
        input_grad[None],
        owned_qkv,
        owned_out,
        grad_w_gate,
        grad_w_up,
        grad_w_down,
        owned_gains[0],
        owned_heads[0],
        owned_heads[1],
        owned_gains[1],
        owned_gains[2],
        owned_gains[3],
    )


def solution(mesh):
    return jax.shard_map(
        local,
        mesh=mesh,
        in_specs=(
            P("dp", "seq", None),
            P("dp", "seq", None),
            P("dp", None),
            P(("seq", "dp"), None),
            P(("seq", "dp"), None),
            P(("seq", "dp"), None),
            P(("seq", "dp"), None),
            P(("seq", "dp"), None),
            P(),
            P(),
            P(),
            P(),
            P(),
            P(),
        ),
        out_specs=(
            P("dp", "seq", None),
            P("dp", "seq", None),
            P(("seq", "dp"), None),
            P(("seq", "dp"), None),
            P(("seq", "dp"), None),
            P(("seq", "dp"), None),
            P(("seq", "dp"), None),
            P(("seq", "dp")),
            P(("seq", "dp")),
            P(("seq", "dp")),
            P(("seq", "dp")),
            P(("seq", "dp")),
            P(("seq", "dp")),
        ),
        check_vma=False,
    )
```

profile of v0, /device:TPU:0, one launch (start us, length us, event | category | flops | bytes accessed | tf_op | source)
XLA Modules:
  0.0 397.0 jit_solution(11133683736897108350)
XLA Ops:
  8.1 4.1 %collective-permute-start = (bf16[1,1,1,1,1,40,768]{6,5,4,3,2,1,0:T(8,128)(2,1)S(1)}, bf16[1,1,1,1,1,40,768]{6,5,4,3,2,1,0:T(8,128)(2,1)S(1)}, u32[]{:S(2)}, u32[]{:S(2)}) collective-permute-start(bf16[1,1,1,1,1,40,768]{6,5,4,3,2,1,0:T(8,128)(2,1)S(1)} %get-tuple-element.78), channel_id=1, source_target_pairs={{0,16},{8,24},{16,0},{24,8},{1,17},{9,25},{17,1},{25,9},{2,18},{10... | collective-permute-start | bytes 184328 | tf_op jit(solution)/shard_map/ppermute | solution.py:29
  12.3 2.8 collective-permute-start.12
  15.2 2.6 pad_maximum_fusion.4
  24.0 2.4 collective-permute-done.1
  30.8 3.6 collective-permute-done.13
  39.8 4.8 %collective-permute-done.14 = bf16[2,2,1,1,1,32,1152]{6,5,4,3,2,1,0:T(8,128)(2,1)S(1)} collective-permute-done((bf16[2,2,1,1,1,32,1152]{6,5,4,3,2,1,0:T(8,128)(2,1)S(1)}, bf16[2,2,1,1,1,32,1152]{6,5,4,3,2,1,0:T(8,128)(2,1)S(1)}, u32[]{:S(2)}, u32[]{:S(2)}) %collective-permute-start.14) | collective-permute-done | bytes 294944 | tf_op jit(solution)/shard_map/ppermute | solution.py:29
  46.9 3.8 collective-permute-done.3
  58.7 3.4 maximum_maximum_fusion
  69.3 3.7 collective-permute-start.10
  73.4 14.9 %collective-permute-done.10 = bf16[1,1,128,512]{3,2,1,0:T(8,128)(2,1)S(1)} collective-permute-done((bf16[1,1,128,512]{3,2,1,0:T(8,128)(2,1)S(1)}, bf16[1,1,128,512]{3,2,1,0:T(8,128)(2,1)S(1)}, u32[]{:S(2)}, u32[]{:S(2)}) %collective-permute-start.10) | collective-permute-done | bytes 131104 | tf_op jit(solution)/shard_map/ppermute | solution.py:29
  88.4 2.8 pad_maximum_fusion.1
  91.3 29.4 %collective-permute-done.11 = bf16[2,1,128,512]{3,2,1,0:T(8,128)(2,1)S(1)} collective-permute-done((bf16[2,1,128,512]{3,2,1,0:T(8,128)(2,1)S(1)}, bf16[2,1,128,512]{3,2,1,0:T(8,128)(2,1)S(1)}, u32[]{:S(2)}, u32[]{:S(2)}) %collective-permute-start.11) | collective-permute-done | bytes 262176 | tf_op jit(solution)/shard_map/ppermute | solution.py:29
  122.8 2.4 multiply_reduce_fusion.9
  128.8 3.4 collective-permute-done.17
  132.2 2.0 collective-permute-start.18
  136.0 4.7 %collective-permute-done.20 = bf16[2,1,128,512]{3,2,1,0:T(8,128)(2,1)S(1)} collective-permute-done((bf16[2,1,128,512]{3,2,1,0:T(8,128)(2,1)S(1)}, bf16[2,1,128,512]{3,2,1,0:T(8,128)(2,1)S(1)}, u32[]{:S(2)}, u32[]{:S(2)}) %collective-permute-start.20) | collective-permute-done | bytes 262176 | tf_op jit(solution)/shard_map/ppermute | solution.py:29
  140.9 2.8 collective-permute-done.21
  145.4 3.4 fusion.69
  148.8 2.5 fusion.71
  151.3 3.0 multiply_convert_fusion.1
  154.3 3.0 fusion.72
  157.8 2.6 collective-permute-done.22
  163.1 6.0 %collective-permute-done.25 = bf16[2,1,128,512]{3,2,1,0:T(8,128)(2,1)S(1)} collective-permute-done((bf16[2,1,128,512]{3,2,1,0:T(8,128)(2,1)S(1)}, bf16[2,1,128,512]{3,2,1,0:T(8,128)(2,1)S(1)}, u32[]{:S(2)}, u32[]{:S(2)}) %collective-permute-start.25) | collective-permute-done | bytes 262176 | tf_op jit(solution)/shard_map/ppermute | solution.py:29
  170.0 2.8 collective-permute-done.23
  174.8 3.5 collective-permute-done.24
  181.4 5.3 %collective-permute-done.27 = bf16[1,1,128,640]{3,2,1,0:T(8,128)(2,1)S(1)} collective-permute-done((bf16[1,1,128,640]{3,2,1,0:T(8,128)(2,1)S(1)}, bf16[1,1,128,640]{3,2,1,0:T(8,128)(2,1)S(1)}, u32[]{:S(2)}, u32[]{:S(2)}) %collective-permute-start.27) | collective-permute-done | bytes 163872 | tf_op jit(solution)/shard_map/ppermute | solution.py:29
  187.3 2.1 collective-permute-start.30
  189.4 4.4 %collective-permute-done.30 = bf16[2,1,128,512]{3,2,1,0:T(8,128)(2,1)S(1)} collective-permute-done((bf16[2,1,128,512]{3,2,1,0:T(8,128)(2,1)S(1)}, bf16[2,1,128,512]{3,2,1,0:T(8,128)(2,1)S(1)}, u32[]{:S(2)}, u32[]{:S(2)}) %collective-permute-start.30) | collective-permute-done | bytes 262176 | tf_op jit(solution)/shard_map/ppermute | solution.py:29
  194.1 2.8 collective-permute-done.31
  197.2 4.8 %multiply_convert_fusion = (bf16[1024,864]{0,1:T(8,128)(2,1)S(1)}, bf16[1024,864]{0,1:T(8,128)(2,1)S(1)}) fusion(f32[1024,864]{0,1:T(8,128)S(1)} %fusion.71, f32[1024,864]{0,1:T(8,128)S(1)} %get-tuple-element.92, bf16[1024,1152]{1,0:T(8,128)(2,1)S(1)} %bitcast.214, bf16[864,1152]{1,0:T(8,128)(2,1)S(1)} %bitcast.221), kind=kOutput, calls=%fused_computation.20 | convolution fusion | flops 2058780672 | bytes 14966784 | tf_op jit(solution)/shard_map/dot_general | solution.py:114
  201.9 2.9 fusion.73
  204.9 3.1 convolution_add_fusion
  208.3 2.5 convolution_convert_fusion.2
  210.8 2.5 convolution_convert_fusion.1
  213.3 2.5 convolution_convert_fusion
  220.8 3.3 pad_maximum_fusion
  224.0 4.1 %collective-permute-done.35 = bf16[2,1,128,512]{3,2,1,0:T(8,128)(2,1)S(1)} collective-permute-done((bf16[2,1,128,512]{3,2,1,0:T(8,128)(2,1)S(1)}, bf16[2,1,128,512]{3,2,1,0:T(8,128)(2,1)S(1)}, u32[]{:S(2)}, u32[]{:S(2)}) %collective-permute-start.35) | collective-permute-done | bytes 262176 | tf_op jit(solution)/shard_map/ppermute | solution.py:29
  232.1 1.8 collective-permute-start.34
  235.1 2.4 collective-permute-done.34
  240.4 2.1 copy-done.2
  247.3 2.4 slice_add_fusion
  253.8 3.4 fusion.25
  261.3 6.8 %collective-permute-done.40 = bf16[2,2,2,1,1,32,1152]{6,5,4,3,2,1,0:T(8,128)(2,1)} collective-permute-done((bf16[2,2,2,1,1,32,1152]{6,5,4,3,2,1,0:T(8,128)(2,1)}, bf16[2,2,2,1,1,32,1152]{6,5,4,3,2,1,0:T(8,128)(2,1)}, u32[]{:S(2)}, u32[]{:S(2)}) %collective-permute-start.40) | collective-permute-done | bytes 589856 | tf_op jit(solution)/shard_map/ppermute | solution.py:29
  272.5 3.0 convolution_bitcast_fusion
  278.2 1.9 slice.704
  282.1 2.1 collective-permute-start.42
  284.2 12.2 %collective-permute-done.37 = bf16[2,1,128,512]{3,2,1,0:T(8,128)(2,1)} collective-permute-done((bf16[2,1,128,512]{3,2,1,0:T(8,128)(2,1)}, bf16[2,1,128,512]{3,2,1,0:T(8,128)(2,1)}, u32[]{:S(2)}, u32[]{:S(2)}) %collective-permute-start.37) | collective-permute-done | bytes 262176 | tf_op jit(solution)/shard_map/ppermute | solution.py:29
  297.5 2.5 collective-permute-start.38
  300.0 8.0 %collective-permute-done.42 = bf16[2,1,1,1,1,32,1152]{6,5,4,3,2,1,0:T(8,128)(2,1)S(1)} collective-permute-done((bf16[2,1,1,1,1,32,1152]{6,5,4,3,2,1,0:T(8,128)(2,1)S(1)}, bf16[2,1,1,1,1,32,1152]{6,5,4,3,2,1,0:T(8,128)(2,1)S(1)}, u32[]{:S(2)}, u32[]{:S(2)}) %collective-permute-start.42) | collective-permute-done | bytes 147488 | tf_op jit(solution)/shard_map/ppermute | solution.py:29
  308.1 2.5 collective-permute-start.43
  310.6 7.3 %collective-permute-done.38 = bf16[1,1,128,512]{3,2,1,0:T(8,128)(2,1)S(1)} collective-permute-done((bf16[1,1,128,512]{3,2,1,0:T(8,128)(2,1)S(1)}, bf16[1,1,128,512]{3,2,1,0:T(8,128)(2,1)S(1)}, u32[]{:S(2)}, u32[]{:S(2)}) %collective-permute-start.38) | collective-permute-done | bytes 131104 | tf_op jit(solution)/shard_map/ppermute | solution.py:29
  317.9 3.2 collective-permute-done.43
  326.9 3.5 fusion.47
  330.5 3.3 multiply_reduce_fusion.2
  336.2 2.6 slice.560
  340.7 2.2 scatter.4
  353.7 7.3 %collective-permute-done.45 = bf16[2,2,1,2,1,40,768]{6,5,4,3,2,1,0:T(8,128)(2,1)S(1)} collective-permute-done((bf16[2,2,1,2,1,40,768]{6,5,4,3,2,1,0:T(8,128)(2,1)S(1)}, bf16[2,2,1,2,1,40,768]{6,5,4,3,2,1,0:T(8,128)(2,1)S(1)}, u32[]{:S(2)}, u32[]{:S(2)}) %collective-permute-start.45) | collective-permute-done | bytes 491552 | tf_op jit(solution)/shard_map/ppermute | solution.py:29
  362.6 2.6 collective-permute-done.50
  366.9 2.9 collective-permute-done.46
  369.9 3.1 collective-permute-start.47
  373.1 2.3 collective-permute-start.52
  375.4 2.1 collective-permute-done.47
  377.6 3.2 collective-permute-start.48
  380.8 2.4 collective-permute-start.53
  (418 shorter events, 121.5 us)
Async XLA Ops:
  7.2 138.2 %all-gather.3.cloned.1.call-start = ((), (), s32[]{:S(2)}) async-start(), calls=%async_computation.1 | async-start | bytes 7464960 | tf_op jit(solution)/shard_map/all_gather | solution.py:218
  8.1 12.0 %collective-permute-start = (bf16[1,1,1,1,1,40,768]{6,5,4,3,2,1,0:T(8,128)(2,1)S(1)}, bf16[1,1,1,1,1,40,768]{6,5,4,3,2,1,0:T(8,128)(2,1)S(1)}, u32[]{:S(2)}, u32[]{:S(2)}) collective-permute-start(bf16[1,1,1,1,1,40,768]{6,5,4,3,2,1,0:T(8,128)(2,1)S(1)} %get-tuple-element.78), channel_id=1, source_target_pairs={{0,16},{8,24},{16,0},{24,8},{1,17},{9,25},{17,1},{25,9},{2,18},{10... | collective-permute-start | bytes 184328 | tf_op jit(solution)/shard_map/ppermute | solution.py:29
  12.2 9.5 %collective-permute-start.5 = (bf16[1,1,1,1,1,40,768]{6,5,4,3,2,1,0:T(8,128)(2,1)S(1)}, bf16[1,1,1,1,1,40,768]{6,5,4,3,2,1,0:T(8,128)(2,1)S(1)}, u32[]{:S(2)}, u32[]{:S(2)}) collective-permute-start(bf16[1,1,1,1,1,40,768]{6,5,4,3,2,1,0:T(8,128)(2,1)S(1)} %get-tuple-element.79), channel_id=1, source_target_pairs={{0,16},{8,24},{16,0},{24,8},{1,17},{9,25},{17,1},{25,9},{2,18},{10... | collective-permute-start | bytes 184328 | tf_op jit(solution)/shard_map/ppermute | solution.py:29
  12.3 10.0 %collective-permute-start.12 = (bf16[1,1,1,1,1,32,1152]{6,5,4,3,2,1,0:T(8,128)(2,1)}, bf16[1,1,1,1,1,32,1152]{6,5,4,3,2,1,0:T(8,128)(2,1)S(1)}, u32[]{:S(2)}, u32[]{:S(2)}) collective-permute-start(bf16[1,1,1,1,1,32,1152]{6,5,4,3,2,1,0:T(8,128)(2,1)} %bitcast.225), channel_id=1, source_target_pairs={{0,16},{8,24},{16,0},{24,8},{1,17},{9,25},{17,1},{25,9},{2,18},{10... | collective-permute-start | bytes 221192 | tf_op jit(solution)/shard_map/ppermute | solution.py:29
  17.8 21.9 %copy-start.8 = (f32[1,128,1152]{2,1,0:T(8,128)S(1)}, f32[1,128,1152]{2,1,0:T(8,128)}, u32[]{:S(2)}) copy-start(f32[1,128,1152]{2,1,0:T(8,128)} %param.16) | copy-start | bytes 1769476
  17.8 368.9 %reduce-scatter.4.cloned.1.call-start = ((), (), s32[]{:S(2)}) async-start(), calls=%async_computation.2 | async-start | bytes 7464960
  20.1 30.6 %copy-start.28 = (bf16[1,1,1,1,1,40,768]{6,5,4,3,2,1,0:T(8,128)(2,1)}, bf16[1,1,1,1,1,40,768]{6,5,4,3,2,1,0:T(8,128)(2,1)S(1)}, u32[]{:S(2)}) copy-start(bf16[1,1,1,1,1,40,768]{6,5,4,3,2,1,0:T(8,128)(2,1)S(1)} %collective-permute-done) | copy-start | bytes 184324
  20.1 6.3 %collective-permute-start.1 = (bf16[2,1,1,1,1,40,768]{6,5,4,3,2,1,0:T(8,128)(2,1)S(1)}, bf16[2,1,1,1,1,40,768]{6,5,4,3,2,1,0:T(8,128)(2,1)S(1)}, u32[]{:S(2)}, u32[]{:S(2)}) collective-permute-start(bf16[2,1,1,1,1,40,768]{6,5,4,3,2,1,0:T(8,128)(2,1)S(1)} %pad_maximum_fusion.29), channel_id=1, source_target_pairs={{0,8},{8,0},{16,24},{24,16},{1,9},{9,1},{17,25},{25,17},{2,10},{10... | collective-permute-start | bytes 368648 | tf_op jit(solution)/shard_map/ppermute | solution.py:29
  21.8 30.0 %copy-start.30 = (bf16[1,1,1,1,1,40,768]{6,5,4,3,2,1,0:T(8,128)(2,1)}, bf16[1,1,1,1,1,40,768]{6,5,4,3,2,1,0:T(8,128)(2,1)S(1)}, u32[]{:S(2)}) copy-start(bf16[1,1,1,1,1,40,768]{6,5,4,3,2,1,0:T(8,128)(2,1)S(1)} %collective-permute-done.5) | copy-start | bytes 184324
  21.8 7.6 %collective-permute-start.6 = (bf16[2,1,1,1,1,40,768]{6,5,4,3,2,1,0:T(8,128)(2,1)S(1)}, bf16[2,1,1,1,1,40,768]{6,5,4,3,2,1,0:T(8,128)(2,1)S(1)}, u32[]{:S(2)}, u32[]{:S(2)}) collective-permute-start(bf16[2,1,1,1,1,40,768]{6,5,4,3,2,1,0:T(8,128)(2,1)S(1)} %pad_maximum_fusion.30), channel_id=1, source_target_pairs={{0,8},{8,0},{16,24},{24,16},{1,9},{9,1},{17,25},{25,17},{2,10},{10... | collective-permute-start | bytes 368648 | tf_op jit(solution)/shard_map/ppermute | solution.py:29
  22.3 35.2 %copy-start.26 = (bf16[1,1,1,1,1,32,1152]{6,5,4,3,2,1,0:T(8,128)(2,1)}, bf16[1,1,1,1,1,32,1152]{6,5,4,3,2,1,0:T(8,128)(2,1)S(1)}, u32[]{:S(2)}) copy-start(bf16[1,1,1,1,1,32,1152]{6,5,4,3,2,1,0:T(8,128)(2,1)S(1)} %collective-permute-done.12) | copy-start | bytes 221188
  22.4 12.0 %collective-permute-start.13 = (bf16[2,1,1,1,1,32,1152]{6,5,4,3,2,1,0:T(8,128)(2,1)S(1)}, bf16[2,1,1,1,1,32,1152]{6,5,4,3,2,1,0:T(8,128)(2,1)S(1)}, u32[]{:S(2)}, u32[]{:S(2)}) collective-permute-start(bf16[2,1,1,1,1,32,1152]{6,5,4,3,2,1,0:T(8,128)(2,1)S(1)} %pad_maximum_fusion.27), channel_id=1, source_target_pairs={{0,8},{8,0},{16,24},{24,16},{1,9},{9,1},{17,25},{25,17},{2,10},{10... | collective-permute-start | bytes 442376 | tf_op jit(solution)/shard_map/ppermute | solution.py:29
  26.4 9.8 %collective-permute-start.2 = (bf16[2,2,1,1,1,40,768]{6,5,4,3,2,1,0:T(8,128)(2,1)S(1)}, bf16[2,2,1,1,1,40,768]{6,5,4,3,2,1,0:T(8,128)(2,1)S(1)}, u32[]{:S(2)}, u32[]{:S(2)}) collective-permute-start(bf16[2,2,1,1,1,40,768]{6,5,4,3,2,1,0:T(8,128)(2,1)S(1)} %pad_maximum_fusion.23), channel_id=1, source_target_pairs={{0,2},{1,3},{2,0},{3,1},{4,6},{5,7},{6,4},{7,5},{8,10},{9,11},{10,... | collective-permute-start | bytes 737288 | tf_op jit(solution)/shard_map/ppermute | solution.py:29
  29.4 8.9 %collective-permute-start.7 = (bf16[2,2,1,1,1,40,768]{6,5,4,3,2,1,0:T(8,128)(2,1)S(1)}, bf16[2,2,1,1,1,40,768]{6,5,4,3,2,1,0:T(8,128)(2,1)S(1)}, u32[]{:S(2)}, u32[]{:S(2)}) collective-permute-start(bf16[2,2,1,1,1,40,768]{6,5,4,3,2,1,0:T(8,128)(2,1)S(1)} %pad_maximum_fusion.24), channel_id=1, source_target_pairs={{0,4},{1,5},{2,6},{3,7},{4,0},{5,1},{6,2},{7,3},{8,12},{9,13},{10,... | collective-permute-start | bytes 737288 | tf_op jit(solution)/shard_map/ppermute | solution.py:29
  34.4 10.2 %collective-permute-start.14 = (bf16[2,2,1,1,1,32,1152]{6,5,4,3,2,1,0:T(8,128)(2,1)S(1)}, bf16[2,2,1,1,1,32,1152]{6,5,4,3,2,1,0:T(8,128)(2,1)S(1)}, u32[]{:S(2)}, u32[]{:S(2)}) collective-permute-start(bf16[2,2,1,1,1,32,1152]{6,5,4,3,2,1,0:T(8,128)(2,1)S(1)} %pad_maximum_fusion.18), channel_id=1, source_target_pairs={{0,4},{1,5},{2,6},{3,7},{4,0},{5,1},{6,2},{7,3},{8,12},{9,13},{10,... | collective-permute-start | bytes 884744 | tf_op jit(solution)/shard_map/ppermute | solution.py:29
  36.2 14.4 %collective-permute-start.3 = (bf16[2,2,1,2,1,40,768]{6,5,4,3,2,1,0:T(8,128)(2,1)S(1)}, bf16[2,2,1,2,1,40,768]{6,5,4,3,2,1,0:T(8,128)(2,1)S(1)}, u32[]{:S(2)}, u32[]{:S(2)}) collective-permute-start(bf16[2,2,1,2,1,40,768]{6,5,4,3,2,1,0:T(8,128)(2,1)S(1)} %pad_maximum_fusion.13), channel_id=1, source_target_pairs={{0,4},{1,5},{2,6},{3,7},{4,0},{5,1},{6,2},{7,3},{8,12},{9,13},{10,... | collective-permute-start | bytes 1474568 | tf_op jit(solution)/shard_map/ppermute | solution.py:29
  38.3 13.4 %collective-permute-start.8 = (bf16[2,2,2,1,1,40,768]{6,5,4,3,2,1,0:T(8,128)(2,1)S(1)}, bf16[2,2,2,1,1,40,768]{6,5,4,3,2,1,0:T(8,128)(2,1)S(1)}, u32[]{:S(2)}, u32[]{:S(2)}) collective-permute-start(bf16[2,2,2,1,1,40,768]{6,5,4,3,2,1,0:T(8,128)(2,1)S(1)} %pad_maximum_fusion.14), channel_id=1, source_target_pairs={{0,2},{1,3},{2,0},{3,1},{4,6},{5,7},{6,4},{7,5},{8,10},{9,11},{10,... | collective-permute-start | bytes 1474568 | tf_op jit(solution)/shard_map/ppermute | solution.py:29
  45.5 12.0 %collective-permute-start.15 = (bf16[2,2,2,1,1,32,1152]{6,5,4,3,2,1,0:T(8,128)(2,1)}, bf16[2,2,2,1,1,32,1152]{6,5,4,3,2,1,0:T(8,128)(2,1)S(1)}, u32[]{:S(2)}, u32[]{:S(2)}) collective-permute-start(bf16[2,2,2,1,1,32,1152]{6,5,4,3,2,1,0:T(8,128)(2,1)} %pad_maximum_fusion.9), channel_id=1, source_target_pairs={{0,2},{1,3},{2,0},{3,1},{4,6},{5,7},{6,4},{7,5},{8,10},{9,11},{10,... | collective-permute-start | bytes 1769480 | tf_op jit(solution)/shard_map/ppermute | solution.py:29
  51.7 6.9 %collective-permute-start.4 = (bf16[2,2,2,2,1,40,768]{6,5,4,3,2,1,0:T(8,128)(2,1)}, bf16[2,2,2,2,1,40,768]{6,5,4,3,2,1,0:T(8,128)(2,1)}, u32[]{:S(2)}, u32[]{:S(2)}) collective-permute-start(bf16[2,2,2,2,1,40,768]{6,5,4,3,2,1,0:T(8,128)(2,1)} %pad_maximum_fusion.7), channel_id=1, source_target_pairs={{0,1},{1,0},{2,3},{3,2},{4,5},{5,4},{6,7},{7,6},{8,9},{9,8},{10,11... | collective-permute-start | bytes 2949128 | tf_op jit(solution)/shard_map/ppermute | solution.py:29
  53.5 5.1 %collective-permute-start.9 = (bf16[2,2,2,2,1,40,768]{6,5,4,3,2,1,0:T(8,128)(2,1)}, bf16[2,2,2,2,1,40,768]{6,5,4,3,2,1,0:T(8,128)(2,1)}, u32[]{:S(2)}, u32[]{:S(2)}) collective-permute-start(bf16[2,2,2,2,1,40,768]{6,5,4,3,2,1,0:T(8,128)(2,1)} %pad_maximum_fusion.8), channel_id=1, source_target_pairs={{0,1},{1,0},{2,3},{3,2},{4,5},{5,4},{6,7},{7,6},{8,9},{9,8},{10,11... | collective-permute-start | bytes 2949128 | tf_op jit(solution)/shard_map/ppermute | solution.py:29
  58.6 29.8 %collective-permute-start.16 = (bf16[2,2,2,2,1,32,1152]{6,5,4,3,2,1,0:T(8,128)(2,1)}, bf16[2,2,2,2,1,32,1152]{6,5,4,3,2,1,0:T(8,128)(2,1)}, u32[]{:S(2)}, u32[]{:S(2)}) collective-permute-start(bf16[2,2,2,2,1,32,1152]{6,5,4,3,2,1,0:T(8,128)(2,1)} %pad_maximum_fusion.5), channel_id=1, source_target_pairs={{0,1},{1,0},{2,3},{3,2},{4,5},{5,4},{6,7},{7,6},{8,9},{9,8},{10,11... | collective-permute-start | bytes 3538952 | tf_op jit(solution)/shard_map/ppermute | solution.py:29
  68.4 20.0 %copy-start.27 = (bf16[1,1,1,1,1,32,1152]{6,5,4,3,2,1,0:T(8,128)(2,1)S(1)}, bf16[1,1,1,1,1,32,1152]{6,5,4,3,2,1,0:T(8,128)(2,1)}, u32[]{:S(2)}) copy-start(bf16[1,1,1,1,1,32,1152]{6,5,4,3,2,1,0:T(8,128)(2,1)} %copy-done.26) | copy-start | bytes 221188
  69.3 19.0 %collective-permute-start.10 = (bf16[1,1,128,512]{3,2,1,0:T(8,128)(2,1)S(1)}, bf16[1,1,128,512]{3,2,1,0:T(8,128)(2,1)S(1)}, u32[]{:S(2)}, u32[]{:S(2)}) collective-permute-start(bf16[1,1,128,512]{3,2,1,0:T(8,128)(2,1)S(1)} %maximum_bitcast_fusion.2), channel_id=1, source_target_pairs={{0,16},{8,24},{16,0},{24,8},{1,17},{9,25},{17,1},{25,9},{2,18},{10... | collective-permute-start | bytes 393224 | tf_op jit(solution)/shard_map/ppermute | solution.py:29
  73.4 47.3 %copy-start.19 = (bf16[128,4,256]{2,0,1:T(8,128)(2,1)}, bf16[128,4,256]{2,0,1:T(8,128)(2,1)S(1)}, u32[]{:S(2)}) copy-start(bf16[128,4,256]{2,0,1:T(8,128)(2,1)S(1)} %fusion.30) | copy-start | bytes 786436
  88.3 32.3 %collective-permute-start.11 = (bf16[2,1,128,512]{3,2,1,0:T(8,128)(2,1)S(1)}, bf16[2,1,128,512]{3,2,1,0:T(8,128)(2,1)S(1)}, u32[]{:S(2)}, u32[]{:S(2)}) collective-permute-start(bf16[2,1,128,512]{3,2,1,0:T(8,128)(2,1)S(1)} %pad_maximum_fusion.19), channel_id=1, source_target_pairs={{0,8},{8,0},{16,24},{24,16},{1,9},{9,1},{17,25},{25,17},{2,10},{10... | collective-permute-start | bytes 786440 | tf_op jit(solution)/shard_map/ppermute | solution.py:29
  91.3 29.8 %copy-start.46 = (pred[128,512]{1,0:T(8,128)(4,1)S(1)}, pred[128,512]{1,0:T(8,128)(4,1)}, u32[]{:S(2)}) copy-start(pred[128,512]{1,0:T(8,128)(4,1)} %fusion.44) | copy-start | bytes 196612
  125.6 6.6 %collective-permute-start.17 = (bf16[1,1,128,640]{3,2,1,0:T(8,128)(2,1)S(1)}, bf16[1,1,128,640]{3,2,1,0:T(8,128)(2,1)S(1)}, u32[]{:S(2)}, u32[]{:S(2)}) collective-permute-start(bf16[1,1,128,640]{3,2,1,0:T(8,128)(2,1)S(1)} %slice_bitcast_fusion.10), channel_id=1, source_target_pairs={{0,2},{1,3},{2,0},{3,1},{4,6},{5,7},{6,4},{7,5},{8,10},{9,11},{10,... | collective-permute-start | bytes 491528 | tf_op jit(solution)/shard_map/ppermute | solution.py:29
  127.2 7.0 %collective-permute-start.19 = (bf16[1,1,128,512]{3,2,1,0:T(8,128)(2,1)S(1)}, bf16[1,1,128,512]{3,2,1,0:T(8,128)(2,1)S(1)}, u32[]{:S(2)}, u32[]{:S(2)}) collective-permute-start(bf16[1,1,128,512]{3,2,1,0:T(8,128)(2,1)S(1)} %slice_bitcast_fusion.12), channel_id=1, source_target_pairs={{0,4},{1,5},{2,6},{3,7},{4,0},{5,1},{6,2},{7,3},{8,12},{9,13},{10,... | collective-permute-start | bytes 393224 | tf_op jit(solution)/shard_map/ppermute | solution.py:29
  132.2 8.5 %collective-permute-start.18 = (bf16[1,2,128,640]{3,2,1,0:T(8,128)(2,1)S(1)}, bf16[1,2,128,640]{3,2,1,0:T(8,128)(2,1)S(1)}, u32[]{:S(2)}, u32[]{:S(2)}) collective-permute-start(bf16[1,2,128,640]{3,2,1,0:T(8,128)(2,1)S(1)} %pad_maximum_fusion.16), channel_id=1, source_target_pairs={{0,4},{1,5},{2,6},{3,7},{4,0},{5,1},{6,2},{7,3},{8,12},{9,13},{10,... | collective-permute-start | bytes 983048 | tf_op jit(solution)/shard_map/ppermute | solution.py:29
  134.2 6.4 %collective-permute-start.20 = (bf16[2,1,128,512]{3,2,1,0:T(8,128)(2,1)S(1)}, bf16[2,1,128,512]{3,2,1,0:T(8,128)(2,1)S(1)}, u32[]{:S(2)}, u32[]{:S(2)}) collective-permute-start(bf16[2,1,128,512]{3,2,1,0:T(8,128)(2,1)S(1)} %pad_maximum_fusion.20), channel_id=1, source_target_pairs={{0,2},{1,3},{2,0},{3,1},{4,6},{5,7},{6,4},{7,5},{8,10},{9,11},{10,... | collective-permute-start | bytes 786440 | tf_op jit(solution)/shard_map/ppermute | solution.py:29
  140.8 2.9 collective-permute-start.21
  157.4 2.9 collective-permute-start.22
  160.7 8.4 %collective-permute-start.25 = (bf16[2,1,128,512]{3,2,1,0:T(8,128)(2,1)S(1)}, bf16[2,1,128,512]{3,2,1,0:T(8,128)(2,1)S(1)}, u32[]{:S(2)}, u32[]{:S(2)}) collective-permute-start(bf16[2,1,128,512]{3,2,1,0:T(8,128)(2,1)S(1)} %slice.526), channel_id=1, source_target_pairs={{0,2},{1,3},{2,0},{3,1},{4,6},{5,7},{6,4},{7,5},{8,10},{9,11},{10,... | collective-permute-start | bytes 786440 | tf_op jit(solution)/shard_map/ppermute | solution.py:29
  162.5 10.4 %collective-permute-start.23 = (bf16[1,2,128,640]{3,2,1,0:T(8,128)(2,1)S(1)}, bf16[1,2,128,640]{3,2,1,0:T(8,128)(2,1)S(1)}, u32[]{:S(2)}, u32[]{:S(2)}) collective-permute-start(bf16[1,2,128,640]{3,2,1,0:T(8,128)(2,1)S(1)} %slice.522), channel_id=1, source_target_pairs={{0,4},{1,5},{2,6},{3,7},{4,0},{5,1},{6,2},{7,3},{8,12},{9,13},{10,... | collective-permute-start | bytes 983048 | tf_op jit(solution)/shard_map/ppermute | solution.py:29
  169.2 5.6 %collective-permute-start.26 = (bf16[1,1,128,512]{3,2,1,0:T(8,128)(2,1)S(1)}, bf16[1,1,128,512]{3,2,1,0:T(8,128)(2,1)S(1)}, u32[]{:S(2)}, u32[]{:S(2)}) collective-permute-start(bf16[1,1,128,512]{3,2,1,0:T(8,128)(2,1)S(1)} %slice.712), channel_id=1, source_target_pairs={{0,4},{1,5},{2,6},{3,7},{4,0},{5,1},{6,2},{7,3},{8,12},{9,13},{10,... | collective-permute-start | bytes 393224 | tf_op jit(solution)/shard_map/ppermute | solution.py:29
  172.9 5.4 %collective-permute-start.24 = (bf16[1,1,128,640]{3,2,1,0:T(8,128)(2,1)S(1)}, bf16[1,1,128,640]{3,2,1,0:T(8,128)(2,1)S(1)}, u32[]{:S(2)}, u32[]{:S(2)}) collective-permute-start(bf16[1,1,128,640]{3,2,1,0:T(8,128)(2,1)S(1)} %slice.708), channel_id=1, source_target_pairs={{0,2},{1,3},{2,0},{3,1},{4,6},{5,7},{6,4},{7,5},{8,10},{9,11},{10,... | collective-permute-start | bytes 491528 | tf_op jit(solution)/shard_map/ppermute | solution.py:29
  180.3 6.3 %collective-permute-start.27 = (bf16[1,1,128,640]{3,2,1,0:T(8,128)(2,1)S(1)}, bf16[1,1,128,640]{3,2,1,0:T(8,128)(2,1)S(1)}, u32[]{:S(2)}, u32[]{:S(2)}) collective-permute-start(bf16[1,1,128,640]{3,2,1,0:T(8,128)(2,1)S(1)} %slice_bitcast_fusion.9), channel_id=1, source_target_pairs={{0,2},{1,3},{2,0},{3,1},{4,6},{5,7},{6,4},{7,5},{8,10},{9,11},{10,... | collective-permute-start | bytes 491528 | tf_op jit(solution)/shard_map/ppermute | solution.py:29
  180.4 6.8 %collective-permute-start.29 = (bf16[1,1,128,512]{3,2,1,0:T(8,128)(2,1)S(1)}, bf16[1,1,128,512]{3,2,1,0:T(8,128)(2,1)S(1)}, u32[]{:S(2)}, u32[]{:S(2)}) collective-permute-start(bf16[1,1,128,512]{3,2,1,0:T(8,128)(2,1)S(1)} %slice_bitcast_fusion.11), channel_id=1, source_target_pairs={{0,4},{1,5},{2,6},{3,7},{4,0},{5,1},{6,2},{7,3},{8,12},{9,13},{10,... | collective-permute-start | bytes 393224 | tf_op jit(solution)/shard_map/ppermute | solution.py:29
  186.7 7.1 %collective-permute-start.28 = (bf16[1,2,128,640]{3,2,1,0:T(8,128)(2,1)S(1)}, bf16[1,2,128,640]{3,2,1,0:T(8,128)(2,1)S(1)}, u32[]{:S(2)}, u32[]{:S(2)}) collective-permute-start(bf16[1,2,128,640]{3,2,1,0:T(8,128)(2,1)S(1)} %pad_maximum_fusion.17), channel_id=1, source_target_pairs={{0,4},{1,5},{2,6},{3,7},{4,0},{5,1},{6,2},{7,3},{8,12},{9,13},{10,... | collective-permute-start | bytes 983048 | tf_op jit(solution)/shard_map/ppermute | solution.py:29
  187.3 6.4 %collective-permute-start.30 = (bf16[2,1,128,512]{3,2,1,0:T(8,128)(2,1)S(1)}, bf16[2,1,128,512]{3,2,1,0:T(8,128)(2,1)S(1)}, u32[]{:S(2)}, u32[]{:S(2)}) collective-permute-start(bf16[2,1,128,512]{3,2,1,0:T(8,128)(2,1)S(1)} %pad_maximum_fusion.21), channel_id=1, source_target_pairs={{0,2},{1,3},{2,0},{3,1},{4,6},{5,7},{6,4},{7,5},{8,10},{9,11},{10,... | collective-permute-start | bytes 786440 | tf_op jit(solution)/shard_map/ppermute | solution.py:29
  194.0 2.9 collective-permute-start.31
  208.1 7.6 %collective-permute-start.32 = (bf16[1,2,2,128,1152]{4,3,2,1,0:T(8,128)(2,1)S(1)}, bf16[1,2,2,128,1152]{4,3,2,1,0:T(8,128)(2,1)S(1)}, u32[]{:S(2)}, u32[]{:S(2)}) collective-permute-start(bf16[1,2,2,128,1152]{4,3,2,1,0:T(8,128)(2,1)S(1)} %bitcast.231), channel_id=1, source_target_pairs={{0,1},{1,0},{2,3},{3,2},{4,5},{5,4},{6,7},{7,6},{8,9},{9,8},{10,11... | collective-permute-start | bytes 3538952 | tf_op jit(solution)/shard_map/ppermute | solution.py:29
  218.3 12.5 %collective-permute-start.33 = (bf16[1,2,128,640]{3,2,1,0:T(8,128)(2,1)}, bf16[1,2,128,640]{3,2,1,0:T(8,128)(2,1)}, u32[]{:S(2)}, u32[]{:S(2)}) collective-permute-start(bf16[1,2,128,640]{3,2,1,0:T(8,128)(2,1)} %slice.534), channel_id=1, source_target_pairs={{0,4},{1,5},{2,6},{3,7},{4,0},{5,1},{6,2},{7,3},{8,12},{9,13},{10,... | collective-permute-start | bytes 983048 | tf_op jit(solution)/shard_map/ppermute | solution.py:29
  219.8 8.3 %collective-permute-start.35 = (bf16[2,1,128,512]{3,2,1,0:T(8,128)(2,1)S(1)}, bf16[2,1,128,512]{3,2,1,0:T(8,128)(2,1)S(1)}, u32[]{:S(2)}, u32[]{:S(2)}) collective-permute-start(bf16[2,1,128,512]{3,2,1,0:T(8,128)(2,1)S(1)} %slice.538), channel_id=1, source_target_pairs={{0,2},{1,3},{2,0},{3,1},{4,6},{5,7},{6,4},{7,5},{8,10},{9,11},{10,... | collective-permute-start | bytes 786440 | tf_op jit(solution)/shard_map/ppermute | solution.py:29
  230.1 5.0 %collective-permute-start.36 = (bf16[1,1,128,512]{3,2,1,0:T(8,128)(2,1)S(1)}, bf16[1,1,128,512]{3,2,1,0:T(8,128)(2,1)S(1)}, u32[]{:S(2)}, u32[]{:S(2)}) collective-permute-start(bf16[1,1,128,512]{3,2,1,0:T(8,128)(2,1)S(1)} %slice.711), channel_id=1, source_target_pairs={{0,4},{1,5},{2,6},{3,7},{4,0},{5,1},{6,2},{7,3},{8,12},{9,13},{10,... | collective-permute-start | bytes 393224 | tf_op jit(solution)/shard_map/ppermute | solution.py:29
  232.1 5.4 %collective-permute-start.34 = (bf16[1,1,128,640]{3,2,1,0:T(8,128)(2,1)S(1)}, bf16[1,1,128,640]{3,2,1,0:T(8,128)(2,1)S(1)}, u32[]{:S(2)}, u32[]{:S(2)}) collective-permute-start(bf16[1,1,128,640]{3,2,1,0:T(8,128)(2,1)S(1)} %slice.707), channel_id=1, source_target_pairs={{0,2},{1,3},{2,0},{3,1},{4,6},{5,7},{6,4},{7,5},{8,10},{9,11},{10,... | collective-permute-start | bytes 491528 | tf_op jit(solution)/shard_map/ppermute | solution.py:29
  243.7 3.6 collective-permute-start.39
  252.0 16.1 %collective-permute-start.40 = (bf16[2,2,2,1,1,32,1152]{6,5,4,3,2,1,0:T(8,128)(2,1)}, bf16[2,2,2,1,1,32,1152]{6,5,4,3,2,1,0:T(8,128)(2,1)}, u32[]{:S(2)}, u32[]{:S(2)}) collective-permute-start(bf16[2,2,2,1,1,32,1152]{6,5,4,3,2,1,0:T(8,128)(2,1)} %slice.700), channel_id=1, source_target_pairs={{0,2},{1,3},{2,0},{3,1},{4,6},{5,7},{6,4},{7,5},{8,10},{9,11},{10,... | collective-permute-start | bytes 1769480 | tf_op jit(solution)/shard_map/ppermute | solution.py:29
  270.1 10.8 %collective-permute-start.41 = (bf16[2,2,1,1,1,32,1152]{6,5,4,3,2,1,0:T(8,128)(2,1)}, bf16[2,2,1,1,1,32,1152]{6,5,4,3,2,1,0:T(8,128)(2,1)}, u32[]{:S(2)}, u32[]{:S(2)}) collective-permute-start(bf16[2,2,1,1,1,32,1152]{6,5,4,3,2,1,0:T(8,128)(2,1)} %slice.703), channel_id=1, source_target_pairs={{0,4},{1,5},{2,6},{3,7},{4,0},{5,1},{6,2},{7,3},{8,12},{9,13},{10,... | collective-permute-start | bytes 884744 | tf_op jit(solution)/shard_map/ppermute | solution.py:29
  280.0 16.4 %collective-permute-start.37 = (bf16[2,1,128,512]{3,2,1,0:T(8,128)(2,1)}, bf16[2,1,128,512]{3,2,1,0:T(8,128)(2,1)}, u32[]{:S(2)}, u32[]{:S(2)}) collective-permute-start(bf16[2,1,128,512]{3,2,1,0:T(8,128)(2,1)} %slice.704), channel_id=1, source_target_pairs={{0,8},{8,0},{16,24},{24,16},{1,9},{9,1},{17,25},{25,17},{2,10},{10... | collective-permute-start | bytes 786440 | tf_op jit(solution)/shard_map/ppermute | solution.py:29
  280.9 41.0 %copy-start.35 = (f32[128,128]{1,0:T(8,128)S(1)}, f32[128,128]{1,0:T(8,128)}, u32[]{:S(2)}) copy-start(f32[128,128]{1,0:T(8,128)} %broadcast_multiply_fusion.3) | copy-start | bytes 196612
  282.1 25.9 %collective-permute-start.42 = (bf16[2,1,1,1,1,32,1152]{6,5,4,3,2,1,0:T(8,128)(2,1)S(1)}, bf16[2,1,1,1,1,32,1152]{6,5,4,3,2,1,0:T(8,128)(2,1)S(1)}, u32[]{:S(2)}, u32[]{:S(2)}) collective-permute-start(bf16[2,1,1,1,1,32,1152]{6,5,4,3,2,1,0:T(8,128)(2,1)S(1)} %slice.709), channel_id=1, source_target_pairs={{0,8},{8,0},{16,24},{24,16},{1,9},{9,1},{17,25},{25,17},{2,10},{10... | collective-permute-start | bytes 442376 | tf_op jit(solution)/shard_map/ppermute | solution.py:29
  297.5 20.4 %collective-permute-start.38 = (bf16[1,1,128,512]{3,2,1,0:T(8,128)(2,1)S(1)}, bf16[1,1,128,512]{3,2,1,0:T(8,128)(2,1)S(1)}, u32[]{:S(2)}, u32[]{:S(2)}) collective-permute-start(bf16[1,1,128,512]{3,2,1,0:T(8,128)(2,1)S(1)} %slice.710), channel_id=1, source_target_pairs={{0,16},{8,24},{16,0},{24,8},{1,17},{9,25},{17,1},{25,9},{2,18},{10... | collective-permute-start | bytes 393224 | tf_op jit(solution)/shard_map/ppermute | solution.py:29
  308.1 13.0 %collective-permute-start.43 = (bf16[1,1,1,1,1,32,1152]{6,5,4,3,2,1,0:T(8,128)(2,1)S(1)}, bf16[1,1,1,1,1,32,1152]{6,5,4,3,2,1,0:T(8,128)(2,1)S(1)}, u32[]{:S(2)}, u32[]{:S(2)}) collective-permute-start(bf16[1,1,1,1,1,32,1152]{6,5,4,3,2,1,0:T(8,128)(2,1)S(1)} %slice.715), channel_id=1, source_target_pairs={{0,16},{8,24},{16,0},{24,8},{1,17},{9,25},{17,1},{25,9},{2,18},{10... | collective-permute-start | bytes 221192 | tf_op jit(solution)/shard_map/ppermute | solution.py:29
  344.7 2.6 collective-permute-start.44
  346.4 2.8 collective-permute-start.49
  347.6 13.3 %collective-permute-start.45 = (bf16[2,2,1,2,1,40,768]{6,5,4,3,2,1,0:T(8,128)(2,1)S(1)}, bf16[2,2,1,2,1,40,768]{6,5,4,3,2,1,0:T(8,128)(2,1)S(1)}, u32[]{:S(2)}, u32[]{:S(2)}) collective-permute-start(bf16[2,2,1,2,1,40,768]{6,5,4,3,2,1,0:T(8,128)(2,1)S(1)} %slice.702), channel_id=1, source_target_pairs={{0,4},{1,5},{2,6},{3,7},{4,0},{5,1},{6,2},{7,3},{8,12},{9,13},{10,... | collective-permute-start | bytes 1474568 | tf_op jit(solution)/shard_map/ppermute | solution.py:29
  351.1 14.2 %collective-permute-start.50 = (bf16[2,2,2,1,1,40,768]{6,5,4,3,2,1,0:T(8,128)(2,1)S(1)}, bf16[2,2,2,1,1,40,768]{6,5,4,3,2,1,0:T(8,128)(2,1)S(1)}, u32[]{:S(2)}, u32[]{:S(2)}) collective-permute-start(bf16[2,2,2,1,1,40,768]{6,5,4,3,2,1,0:T(8,128)(2,1)S(1)} %slice.701), channel_id=1, source_target_pairs={{0,2},{1,3},{2,0},{3,1},{4,6},{5,7},{6,4},{7,5},{8,10},{9,11},{10,... | collective-permute-start | bytes 1474568 | tf_op jit(solution)/shard_map/ppermute | solution.py:29
  361.1 8.7 %collective-permute-start.46 = (bf16[2,2,1,1,1,40,768]{6,5,4,3,2,1,0:T(8,128)(2,1)S(1)}, bf16[2,2,1,1,1,40,768]{6,5,4,3,2,1,0:T(8,128)(2,1)S(1)}, u32[]{:S(2)}, u32[]{:S(2)}) collective-permute-start(bf16[2,2,1,1,1,40,768]{6,5,4,3,2,1,0:T(8,128)(2,1)S(1)} %slice.706), channel_id=1, source_target_pairs={{0,2},{1,3},{2,0},{3,1},{4,6},{5,7},{6,4},{7,5},{8,10},{9,11},{10,... | collective-permute-start | bytes 737288 | tf_op jit(solution)/shard_map/ppermute | solution.py:29
  365.4 7.6 %collective-permute-start.51 = (bf16[2,2,1,1,1,40,768]{6,5,4,3,2,1,0:T(8,128)(2,1)S(1)}, bf16[2,2,1,1,1,40,768]{6,5,4,3,2,1,0:T(8,128)(2,1)S(1)}, u32[]{:S(2)}, u32[]{:S(2)}) collective-permute-start(bf16[2,2,1,1,1,40,768]{6,5,4,3,2,1,0:T(8,128)(2,1)S(1)} %slice.705), channel_id=1, source_target_pairs={{0,4},{1,5},{2,6},{3,7},{4,0},{5,1},{6,2},{7,3},{8,12},{9,13},{10,... | collective-permute-start | bytes 737288 | tf_op jit(solution)/shard_map/ppermute | solution.py:29
  369.9 7.6 %collective-permute-start.47 = (bf16[2,1,1,1,1,40,768]{6,5,4,3,2,1,0:T(8,128)(2,1)S(1)}, bf16[2,1,1,1,1,40,768]{6,5,4,3,2,1,0:T(8,128)(2,1)S(1)}, u32[]{:S(2)}, u32[]{:S(2)}) collective-permute-start(bf16[2,1,1,1,1,40,768]{6,5,4,3,2,1,0:T(8,128)(2,1)S(1)} %slice.714), channel_id=1, source_target_pairs={{0,8},{8,0},{16,24},{24,16},{1,9},{9,1},{17,25},{25,17},{2,10},{10... | collective-permute-start | bytes 368648 | tf_op jit(solution)/shard_map/ppermute | solution.py:29
  373.1 7.6 %collective-permute-start.52 = (bf16[2,1,1,1,1,40,768]{6,5,4,3,2,1,0:T(8,128)(2,1)S(1)}, bf16[2,1,1,1,1,40,768]{6,5,4,3,2,1,0:T(8,128)(2,1)S(1)}, u32[]{:S(2)}, u32[]{:S(2)}) collective-permute-start(bf16[2,1,1,1,1,40,768]{6,5,4,3,2,1,0:T(8,128)(2,1)S(1)} %slice.713), channel_id=1, source_target_pairs={{0,8},{8,0},{16,24},{24,16},{1,9},{9,1},{17,25},{25,17},{2,10},{10... | collective-permute-start | bytes 368648 | tf_op jit(solution)/shard_map/ppermute | solution.py:29
  377.6 7.0 %collective-permute-start.48 = (bf16[1,1,1,1,1,40,768]{6,5,4,3,2,1,0:T(8,128)(2,1)S(1)}, bf16[1,1,1,1,1,40,768]{6,5,4,3,2,1,0:T(8,128)(2,1)S(1)}, u32[]{:S(2)}, u32[]{:S(2)}) collective-permute-start(bf16[1,1,1,1,1,40,768]{6,5,4,3,2,1,0:T(8,128)(2,1)S(1)} %slice.719), channel_id=1, source_target_pairs={{0,16},{8,24},{16,0},{24,8},{1,17},{9,25},{17,1},{25,9},{2,18},{10... | collective-permute-start | bytes 184328 | tf_op jit(solution)/shard_map/ppermute | solution.py:29
  380.8 5.2 %collective-permute-start.53 = (bf16[1,1,1,1,1,40,768]{6,5,4,3,2,1,0:T(8,128)(2,1)S(1)}, bf16[1,1,1,1,1,40,768]{6,5,4,3,2,1,0:T(8,128)(2,1)S(1)}, u32[]{:S(2)}, u32[]{:S(2)}) collective-permute-start(bf16[1,1,1,1,1,40,768]{6,5,4,3,2,1,0:T(8,128)(2,1)S(1)} %slice.718), channel_id=1, source_target_pairs={{0,16},{8,24},{16,0},{24,8},{1,17},{9,25},{17,1},{25,9},{2,18},{10... | collective-permute-start | bytes 184328 | tf_op jit(solution)/shard_map/ppermute | solution.py:29
  (71 other events, 373.3 us)
Sparse Core Ops, SparseCore 0:
  17.9 117.1 all-gather.2
  258.6 118.8 reduce-scatter.3
where the time goes:
time: 403 us; the launch traced here: 397 us
  waiting for transfers between devices  165 us (41%)
  starting transfers between devices  69.8 us (17%)
  other arithmetic  55 us (14%)
  matrix products  51.3 us (13%)
  local copies, waits for them, and re-layouts  39.9 us (10%)
  between operations  16.1 us (4%)
    ppermute x54, waiting for transfers between devices, swapped(): return lax.ppermute(value, axis, [(i, i ^ bit) for i in range(length)])  165 us
    ppermute x54, starting transfers between devices, swapped(): return lax.ppermute(value, axis, [(i, i ^ bit) for i in range(length)])  69.7 us
    dot_general x5, matrix products, contract_cols(): lax.dot_general(left, right, (((1,), (1,)), ((), ())), preferred_element_...  17.2 us
    dot_general x7, matrix products, dot32(): return jnp.dot(left, right, preferred_element_type=jnp.float32)  14.3 us
    add x18, other arithmetic, keep_half(): own.astype(jnp.float32) + swapped(other, axis, bit).astype(jnp.float32)  10.8 us
    slice x27, local copies, waits for them, and re-layouts, keep_half(): other = lax.slice_in_dim(value, 1, 2, axis=at).astype(jnp.bfloat16)  9.6 us
    unnamed x156, local copies, waits for them, and re-layouts  9.56 us
    dot_general x5, matrix products, contract_rows(): lax.dot_general(left, right, (((0,), (0,)), ((), ())), preferred_element_...  9.39 us
  transfers between devices with their start and end apart: 56, of which 37 were waited for; matrix products, arithmetic and copies ran while one was open for 24% of the time, Pallas kernels for 0%

commit v1 on v0

v1 whole, which is shorter than its diff:
```python
import math

import functools

import jax
import jax.numpy as jnp
from jax import lax
from jax.experimental import pallas as pl
from jax.experimental.pallas import tpu as pltpu
from jax.sharding import PartitionSpec as P

HEADS = 4
HEAD_DIM = 256
WINDOW = 512


EPSILON = 1e-06
GELU_SLOPE = math.sqrt(2.0 / math.pi)
GELU_CUBIC = 0.044715


def bits_of(count):
    bits = []
    bit = 1
    while bit < count:
        bits.append(bit)
        bit *= 2
    return bits


def swapped(value, axis, bit):
    length = lax.axis_size(axis)
    return lax.ppermute(value, axis, [(i, i ^ bit) for i in range(length)])


def one_hot_order(origin, count):
    return (jnp.arange(count, dtype=jnp.int32)[:, None] == origin[None, :]).astype(jnp.bfloat16)


def in_order(value, order):
    high = value.astype(jnp.bfloat16)
    low = (value - high.astype(jnp.float32)).astype(jnp.bfloat16)
    return contract_cols(high, order) + contract_cols(low, order)


def inv_root(vector):
    return lax.rsqrt(jnp.mean(vector * vector, axis=-1, keepdims=True) + EPSILON)


def norm_back(grad, unit_part, root_part, gain):
    scaled = grad * gain
    return root_part * (scaled - unit_part * jnp.mean(scaled * unit_part, axis=-1, keepdims=True))


def gelu_pair(gate):
    inner = jnp.tanh(GELU_SLOPE * (gate + GELU_CUBIC * gate * gate * gate))
    gelu_value = 0.5 * gate * (1.0 + inner)
    gelu_slope = 0.5 * (1.0 + inner) + 0.5 * gate * (1.0 - inner * inner) * GELU_SLOPE * (
        1.0 + 3.0 * GELU_CUBIC * gate * gate
    )
    return (gelu_value, gelu_slope)


def turn_half(vector):
    half = vector.shape[-1] // 2
    return jnp.concatenate([-vector[..., half:], vector[..., :half]], axis=-1)


def seq_begin(index, starts):
    return jnp.max(jnp.where(starts[None, :] <= index[:, None], starts[None, :], 0), axis=1)


def rope_tables(position, head):
    freq = jnp.exp(-math.log(10000.0) * jnp.arange(head // 2, dtype=jnp.float32) * (2.0 / head))
    angle = position[:, None] * freq[None, :]
    angle = jnp.concatenate([angle, angle], axis=1)
    return (jnp.cos(angle), jnp.sin(angle))


def dot32(left, right):
    return jnp.dot(left, right, preferred_element_type=jnp.float32)


def contract_rows(left, right):
    return lax.dot_general(
        left, right, (((0,), (0,)), ((), ())), preferred_element_type=jnp.float32
    )


def contract_cols(left, right):
    return lax.dot_general(
        left, right, (((1,), (1,)), ((), ())), preferred_element_type=jnp.float32
    )


MESH = pl.DeviceIdType.MESH


def group_width(dp_count):
    return dp_count // 2


def flip(value, other, count):
    if count & (count - 1):
        return (value + other) % count
    total = 0
    for bit in bits_of(count):
        total = total + ((value // bit + other // bit) % 2) * bit
    return total


def column_tiles(width):
    best = 128
    for size in range(128, 513, 128):
        if width % size == 0:
            best = size
    return [slice(at, at + best) for at in range(0, width, best)]


def nt(left, right):
    return lax.dot_general(left, right, (((1,), (1,)), ((), ())), preferred_element_type=jnp.float32)


def tn(left, right):
    return lax.dot_general(left, right, (((0,), (0,)), ((), ())), preferred_element_type=jnp.float32)


def ffn_kernel(zs, ys, ws, rows, width, own, *refs):
    half = ws // 2
    x_ref, hidden_ref, grad_ref, gain_ref = refs[:4]
    w_refs = refs[4 : 4 + 3 * half]
    result_ref, gg_ref, in_grad_ref, kept_ref = refs[4 + 3 * half : 8 + 3 * half]
    at = 8 + 3 * half
    passed_ref = None
    if half > 1:
        passed_ref = refs[at]
        at += 1
    (tok, grd, wt, gate, up, hid, dgb, dub, acc, part, grad_own, ysend, yrecv, zsend, zrecv, dwsend, dwrecv) = refs[
        at : at + 17
    ]
    (agz_s, agy_s, ag_r, ry_s, ry_r, rz_s, rz_r, wl_s, wr_s, wr_r, dw_s, dw_r) = refs[at + 17 :]
    z = lax.axis_index("seq")
    d = lax.axis_index("dp")
    y = d // ws
    w = d % ws
    mate = y * ws + w + 1 - 2 * (w % 2)
    pair = ys * rows
    tiles = column_tiles(width)

    def peer(zz, yy):
        return (zz, yy * ws + w)

    def block(zz, yy):
        return pl.ds(pl.multiple_of((zz * ys + yy) * rows, rows), rows)

    def span(zz):
        return pl.ds(pl.multiple_of(zz * pair, pair), pair)

    barrier = pltpu.get_barrier_semaphore()
    for dz in range(1, zs):
        pl.semaphore_signal(barrier, inc=1, device_id=peer(flip(z, dz, zs), y), device_id_type=MESH)
    for dy in range(1, ys):
        pl.semaphore_signal(barrier, inc=1, device_id=peer(z, (y + dy) % ys), device_id_type=MESH)
    pl.semaphore_signal(barrier, inc=1, device_id=(z, mate), device_id_type=MESH)
    for i in range(half):
        for m in range(3):
            pltpu.make_async_copy(w_refs[3 * i + m], wt.at[m, 2 * i], wl_s.at[i, m]).start()
    pl.semaphore_wait(barrier, zs + ys - 1)

    def copy_z(p, src, buf, dz):
        return pltpu.make_async_remote_copy(
            src_ref=src,
            dst_ref=buf.at[block(z, y)],
            send_sem=agz_s.at[p, dz],
            recv_sem=ag_r.at[p, z, y],
            device_id=peer(flip(z, dz, zs), y),
            device_id_type=MESH,
        )

    def copy_y(p, src, buf, zz, dy):
        return pltpu.make_async_remote_copy(
            src_ref=src,
            dst_ref=buf.at[block(zz, y)],
            send_sem=agy_s.at[p, zz, dy],
            recv_sem=ag_r.at[p, zz, y],
            device_id=peer(z, (y + dy) % ys),
            device_id_type=MESH,
        )

    def arrived(p, buf, zz, yy):
        pltpu.make_async_remote_copy(
            src_ref=buf.at[block(zz, yy)],
            dst_ref=buf.at[block(zz, yy)],
            send_sem=agz_s.at[p, 0],
            recv_sem=ag_r.at[p, zz, yy],
            device_id=peer(z, y),
            device_id_type=MESH,
        ).wait_recv()

    def copy_wide(i, m):
        return pltpu.make_async_remote_copy(
            src_ref=w_refs[3 * i + m],
            dst_ref=wt.at[m, 2 * i + 1],
            send_sem=wr_s.at[i, m],
            recv_sem=wr_r.at[i, m],
            device_id=(z, mate),
            device_id_type=MESH,
        )

    def reduce_y(p, zz, dy):
        return pltpu.make_async_remote_copy(
            src_ref=ysend.at[dy - 1, zz],
            dst_ref=yrecv.at[ys - dy - 1, zz],
            send_sem=ry_s.at[p, dy - 1, zz],
            recv_sem=ry_r.at[p, ys - dy - 1, zz],
            device_id=peer(z, (y + dy) % ys),
            device_id_type=MESH,
        )

    def reduce_z(p, zz):
        return pltpu.make_async_remote_copy(
            src_ref=zsend.at[zz],
            dst_ref=zrecv.at[z],
            send_sem=rz_s.at[p, zz],
            recv_sem=rz_r.at[p, z],
            device_id=peer(zz, y),
            device_id_type=MESH,
        )

    def reduced(p, zz):
        return pltpu.make_async_remote_copy(
            src_ref=zsend.at[zz],
            dst_ref=zrecv.at[zz],
            send_sem=rz_s.at[p, zz],
            recv_sem=rz_r.at[p, zz],
            device_id=peer(z, y),
            device_id_type=MESH,
        )

    def combine(p, zz, mine):
        total = part[zz]
        for dy in range(1, ys):
            reduce_y(p, zz, dy).wait_recv()
            total = total + yrecv[ys - dy - 1, zz].astype(jnp.float32)
        if mine:
            part[zz] = total
        else:
            zsend[zz] = total.astype(jnp.bfloat16)
            reduce_z(p, zz).start()

    def phase(p, src, buf, compute, ready, between):
        for dy in range(1, ys):
            copy_y(p, src, buf, z, dy).start()
        for dz in range(1, zs):
            copy_z(p, src, buf, dz).start()
        buf[block(z, y), :] = src[...]
        ready()

        def step(dz, carry):
            zz = flip(z, dz, zs)

            @pl.when(dz + 1 < zs)
            def _():
                nxt = flip(z, dz + 1, zs)
                arrived(p, buf, nxt, y)
                for dy in range(1, ys):
                    copy_y(p, buf.at[block(nxt, y)], buf, nxt, dy).start()

            for dy in range(1, ys):
                arrived(p, buf, zz, (y + dy) % ys)
            compute(zz)
            for dy in range(1, ys):
                yy = (y + dy) % ys
                ysend[dy - 1, zz] = acc[pl.ds(pl.multiple_of(yy * rows, rows), rows), :].astype(jnp.bfloat16)
                reduce_y(p, zz, dy).start()
            part[zz] = acc[pl.ds(pl.multiple_of(y * rows, rows), rows), :]

            @pl.when(dz == 1)
            def _():
                combine(p, z, True)

            @pl.when(dz > 1)
            def _():
                combine(p, flip(z, dz - 1, zs), False)

            return carry

        lax.fori_loop(0, zs, step, 0)
        combine(p, flip(z, zs - 1, zs), zs == 1)
        between()
        total = part[z]
        for dz in range(1, zs):
            zz = flip(z, dz, zs)
            reduced(p, zz).wait_recv()
            total = total + zrecv[zz].astype(jnp.float32)
        return total

    def sent(p, src, buf):
        for dz in range(1, zs):
            copy_z(p, src, buf, dz).wait_send()
            reduce_z(p, flip(z, dz, zs)).wait_send()
        for zz in range(zs):
            for dy in range(1, ys):
                copy_y(p, src, buf, zz, dy).wait_send()
                reduce_y(p, zz, dy).wait_send()

    def forward(zz):
        acc[...] = jnp.zeros_like(acc)

        def shard(s, carry):
            x = tok[span(zz), :]
            gate_part = nt(x, wt[0, s])
            up_part = nt(x, wt[1, s])
            gate[s, span(zz), :] = gate_part
            up[s, span(zz), :] = up_part
            inner = jnp.tanh(GELU_SLOPE * (gate_part + GELU_CUBIC * gate_part * gate_part * gate_part))
            hidden = (0.5 * gate_part * (1.0 + inner) * up_part).astype(jnp.bfloat16)
            hid[s, span(zz), :] = hidden
            for tile in tiles:
                acc[:, tile] = acc[:, tile] + dot32(hidden, wt[2, s, :, tile])
            return carry

        lax.fori_loop(0, ws, shard, 0)

    def backward(zz):
        acc[...] = jnp.zeros_like(acc)

        def shard(s, carry):
            hidden_grad = nt(grd[span(zz), :], wt[2, s])
            gelu_value, gelu_slope = gelu_pair(gate[s, span(zz), :])
            dgate = (hidden_grad * up[s, span(zz), :] * gelu_slope).astype(jnp.bfloat16)
            dup = (hidden_grad * gelu_value).astype(jnp.bfloat16)
            dgb[s, span(zz), :] = dgate
            dub[s, span(zz), :] = dup
            for tile in tiles:
                acc[:, tile] = acc[:, tile] + dot32(dgate, wt[0, s, :, tile]) + dot32(dup, wt[1, s, :, tile])
            return carry

        lax.fori_loop(0, ws, shard, 0)

    def weights_ready():
        for i in range(half):
            for m in range(3):
                pltpu.make_async_copy(w_refs[3 * i + m], wt.at[m, 2 * i], wl_s.at[i, m]).wait()
        for i in range(half):
            for m in range(3):
                copy_wide(i, m).wait_recv()

    def nothing():
        return None

    def copy_dw(i, m):
        return pltpu.make_async_remote_copy(
            src_ref=dwsend.at[i, m],
            dst_ref=dwrecv.at[i, m],
            send_sem=dw_s.at[i, m],
            recv_sem=dw_r.at[i, m],
            device_id=(z, mate),
            device_id_type=MESH,
        )

    terms = ((dgb, tok), (dub, tok), (hid, grd))

    def weight_terms():
        for m in range(3):
            left, right = terms[m]

            def away(i, carry):
                for tile in tiles:
                    dwsend[i, m, :, tile] = tn(left[2 * i + 1], right[:, tile]).astype(jnp.bfloat16)
                copy_dw(i, m).start()
                return carry

            lax.fori_loop(0, half, away, 0)
        for m in range(3):
            left, right = terms[m]

            def home(i, carry):
                copy_dw(i, m).wait_recv()
                for tile in tiles:
                    total = tn(left[2 * i], right[:, tile]) + dwrecv[i, m, :, tile].astype(jnp.float32)

                    @pl.when(i == 0)
                    def _():
                        kept_ref[m, :, tile] = total

                    if half > 1:

                        @pl.when(i > 0)
                        def _():
                            passed_ref[jnp.maximum(i - 1, 0), m, :, tile] = total.astype(jnp.bfloat16)

                return carry

            lax.fori_loop(0, half, home, 0)

    for i in range(half):
        for m in range(3):
            copy_wide(i, m).start()
    ffn_out = phase(0, x_ref, tok, forward, weights_ready, nothing)
    root = inv_root(ffn_out)
    unit = ffn_out * root
    gain = gain_ref[...]
    result_ref[...] = hidden_ref[...] + unit * gain
    rows_grad = grad_ref[...]
    gg_ref[...] = jnp.sum(rows_grad * unit, axis=0, keepdims=True)
    grad_own[...] = norm_back(rows_grad, unit, root, gain).astype(jnp.bfloat16)
    sent(0, x_ref, tok)
    in_grad_ref[...] = phase(1, grad_own, grd, backward, nothing, weight_terms)

    for i in range(half):
        for m in range(3):
            copy_wide(i, m).wait_send()
            copy_dw(i, m).wait_send()
    sent(1, grad_own, grd)


def ffn_block(ffn_input, hidden_in, rows_grad, gain, ffn_rows, zs, dp_count):
    rows, width = ffn_input.shape
    own = ffn_rows[0][0].shape[0]
    ws = group_width(dp_count)
    ys = dp_count // ws
    half = ws // 2
    tokens = zs * ys * rows
    bf, f32 = jnp.bfloat16, jnp.float32
    vmem = pl.BlockSpec(memory_space=pltpu.VMEM)
    outs = [
        jax.ShapeDtypeStruct((rows, width), f32),
        jax.ShapeDtypeStruct((1, width), f32),
        jax.ShapeDtypeStruct((rows, width), f32),
        jax.ShapeDtypeStruct((3, own, width), f32),
    ]
    if half > 1:
        outs.append(jax.ShapeDtypeStruct((half - 1, 3, own, width), bf))
    dma = pltpu.SemaphoreType.DMA
    scratch = [
        pltpu.VMEM((tokens, width), bf),
        pltpu.VMEM((tokens, width), bf),
        pltpu.VMEM((3, ws, own, width), bf),
        pltpu.VMEM((ws, tokens, own), f32),
        pltpu.VMEM((ws, tokens, own), f32),
        pltpu.VMEM((ws, tokens, own), bf),
        pltpu.VMEM((ws, tokens, own), bf),
        pltpu.VMEM((ws, tokens, own), bf),
        pltpu.VMEM((ys * rows, width), f32),
        pltpu.VMEM((zs, rows, width), f32),
        pltpu.VMEM((rows, width), bf),
        pltpu.VMEM((ys - 1, zs, rows, width), bf),
        pltpu.VMEM((ys - 1, zs, rows, width), bf),
        pltpu.VMEM((zs, rows, width), bf),
        pltpu.VMEM((zs, rows, width), bf),
        pltpu.VMEM((half, 3, own, width), bf),
        pltpu.VMEM((half, 3, own, width), bf),
        dma((2, zs)),
        dma((2, zs, ys)),
        dma((2, zs, ys)),
        dma((2, ys - 1, zs)),
        dma((2, ys - 1, zs)),
        dma((2, zs)),
        dma((2, zs)),
        dma((half, 3)),
        dma((half, 3)),
        dma((half, 3)),
        dma((half, 3)),
        dma((half, 3)),
    ]
    flat = [w for group in ffn_rows for w in group]
    flops = 2 * tokens * ws * own * width * 9
    out = pl.pallas_call(
        functools.partial(ffn_kernel, zs, ys, ws, rows, width, own),
        out_shape=outs,
        in_specs=[vmem] * 4 + [pl.BlockSpec(memory_space=pl.ANY)] * len(flat),
        out_specs=[vmem] * len(outs),
        scratch_shapes=scratch,
        compiler_params=pltpu.CompilerParams(
            collective_id=1, has_side_effects=True, vmem_limit_bytes=67043328
        ),
        cost_estimate=pl.CostEstimate(flops=flops, bytes_accessed=40 << 20, transcendentals=0),
        name="ffn_block",
    )(ffn_input, hidden_in, rows_grad, gain[None, :], *flat)
    passed = out[4] if half > 1 else None
    return out[0], out[1], out[2], out[3], passed


def spread_kernel(zs, ys, xs, width, cut, with_kv, *refs):
    refs = list(refs)
    w_ref = refs.pop(0)
    kv_ref = refs.pop(0) if with_kv else None
    out_ref = refs.pop(0)
    kv_out = refs.pop(0) if with_kv else None
    own_s, z_s, far_s, far_r = refs[:4]
    kv_own, kv_s, kv_r = refs[4:7] if with_kv else (None, None, None)
    z = lax.axis_index("seq")
    d = lax.axis_index("dp")
    y, x, c = d // (2 * xs), (d // 2) % xs, d % 2
    cols = (pl.ds(0, cut), pl.ds(cut, width - cut))

    def dev(zz, yy, xx, cc):
        return (zz, (yy * xs + xx) * 2 + cc)

    barrier = pltpu.get_barrier_semaphore()
    near = [dev(flip(z, dz, zs), y, x, c) for dz in range(1, zs)]
    near += [dev(z, (y + dy) % ys, x, c) for dy in range(1, ys)]
    near += [dev(z, y, (x + dx) % xs, c) for dx in range(1, xs)]
    near += [dev(z, y, x, 1 - c)]
    for peer in near:
        pl.semaphore_signal(barrier, inc=1, device_id=peer, device_id_type=MESH)
    pl.semaphore_wait(barrier, len(near))

    def slot(h, zz, yy, xx, cc):
        return out_ref.at[zz, yy, xx, cc, :, cols[h]]

    def copy(h, src, zz, yy, xx, send, to):
        return pltpu.make_async_remote_copy(
            src_ref=src,
            dst_ref=slot(h, zz, yy, xx, c),
            send_sem=send,
            recv_sem=far_r.at[h, zz, yy, xx, c],
            device_id=to,
            device_id_type=MESH,
        )

    def along(h, dz):
        return copy(h, w_ref.at[:, cols[h]], z, y, x, z_s.at[h, dz], dev(flip(z, dz, zs), y, x, c))

    def over_y(h, src, zz, yy, xx, dy):
        return copy(h, src, zz, yy, xx, far_s.at[h, zz, yy, xx, dy], dev(z, (y + dy) % ys, x, c))

    def over_x(h, src, zz, yy, xx, dx):
        return copy(h, src, zz, yy, xx, far_s.at[h, zz, yy, xx, ys - 1 + dx], dev(z, y, (x + dx) % xs, c))

    def over_core(h, src, zz, yy, xx):
        return copy(h, src, zz, yy, xx, far_s.at[h, zz, yy, xx, 0], dev(z, y, x, 1 - c))

    def arrived(h, zz, yy, xx, cc):
        pltpu.make_async_remote_copy(
            src_ref=slot(h, zz, yy, xx, cc),
            dst_ref=slot(h, zz, yy, xx, cc),
            send_sem=z_s.at[h, 0],
            recv_sem=far_r.at[h, zz, yy, xx, cc],
            device_id=dev(z, y, x, 1 - c),
            device_id_type=MESH,
        ).wait_recv()

    def kv_copy(dz):
        return pltpu.make_async_remote_copy(
            src_ref=kv_ref,
            dst_ref=kv_out.at[z],
            send_sem=kv_s.at[dz],
            recv_sem=kv_r.at[z],
            device_id=dev(flip(z, dz, zs), y, x, c),
            device_id_type=MESH,
        )

    def kv_arrived(zz):
        pltpu.make_async_remote_copy(
            src_ref=kv_ref,
            dst_ref=kv_out.at[zz],
            send_sem=kv_s.at[0],
            recv_sem=kv_r.at[zz],
            device_id=dev(z, y, x, 1 - c),
            device_id_type=MESH,
        ).wait_recv()

    def onward(h, src, zz):
        if h == 0:
            for dy in range(1, ys):
                over_y(h, src, zz, y, x, dy).start()
        for dx in range(1, xs):
            over_x(h, src, zz, y, x, dx).start()
        if h == 1:
            for dy in range(1, ys):
                over_y(h, src, zz, y, x, dy).start()
        over_core(h, src, zz, y, x).start()

    if with_kv:
        for dz in range(1, zs):
            kv_copy(dz).start()
    for dz in range(1, zs):
        for h in range(2):
            along(h, dz).start()
    for h in range(2):
        onward(h, w_ref.at[:, cols[h]], z)
    keep = pltpu.make_async_copy(w_ref, out_ref.at[z, y, x, c], own_s.at[0])
    keep.start()
    if with_kv:
        kv_keep = pltpu.make_async_copy(kv_ref, kv_out.at[z], kv_own.at[0])
        kv_keep.start()

    def step(t, carry):
        @pl.when(t < zs)
        def _():
            zz = flip(z, t, zs)
            for h in range(2):

                @pl.when(t > 0)
                def _():
                    arrived(h, zz, y, x, c)
                    onward(h, slot(h, zz, y, x, c), zz)

        @pl.when(jnp.logical_and(t >= 1, t < zs + 1))
        def _():
            zz = flip(z, t - 1, zs)
            for dy in range(1, ys):
                yy = (y + dy) % ys
                arrived(0, zz, yy, x, c)
                for dx in range(1, xs):
                    over_x(0, slot(0, zz, yy, x, c), zz, yy, x, dx).start()
                over_core(0, slot(0, zz, yy, x, c), zz, yy, x).start()
            for dx in range(1, xs):
                xx = (x + dx) % xs
                arrived(1, zz, y, xx, c)
                for dy in range(1, ys):
                    over_y(1, slot(1, zz, y, xx, c), zz, y, xx, dy).start()
                over_core(1, slot(1, zz, y, xx, c), zz, y, xx).start()

        @pl.when(t >= 2)
        def _():
            zz = flip(z, t - 2, zs)
            for dx in range(1, xs):
                xx = (x + dx) % xs
                for dy in range(ys):
                    yy = (y + dy) % ys
                    arrived(0, zz, yy, xx, c)
                    over_core(0, slot(0, zz, yy, xx, c), zz, yy, xx).start()
            for dy in range(1, ys):
                yy = (y + dy) % ys
                for dx in range(xs):
                    xx = (x + dx) % xs
                    arrived(1, zz, yy, xx, c)
                    over_core(1, slot(1, zz, yy, xx, c), zz, yy, xx).start()

        return carry

    lax.fori_loop(0, zs + 2, step, 0)

    def settle(zz, carry):
        for yy in range(ys):
            for xx in range(xs):
                for h in range(2):
                    arrived(h, zz, yy, xx, 1 - c)
                    over_core(h, slot(h, zz, yy, xx, c), zz, yy, xx).wait_send()
        for dx in range(1, xs):
            for dy in range(ys):
                yy = (y + dy) % ys
                over_x(0, slot(0, zz, yy, x, c), zz, yy, x, dx).wait_send()
            over_x(1, slot(1, zz, y, x, c), zz, y, x, dx).wait_send()
        for dy in range(1, ys):
            for dx in range(xs):
                xx = (x + dx) % xs
                over_y(1, slot(1, zz, y, xx, c), zz, y, xx, dy).wait_send()
            over_y(0, slot(0, zz, y, x, c), zz, y, x, dy).wait_send()
        return carry

    lax.fori_loop(0, zs, settle, 0)
    keep.wait()
    for dz in range(1, zs):
        for h in range(2):
            along(h, dz).wait_send()
    if with_kv:
        kv_keep.wait()
        for dz in range(1, zs):
            kv_arrived(flip(z, dz, zs))
            kv_copy(dz).wait_send()


def half_columns(width):
    return (width // 256) * 128 + (128 if width % 256 else 0)


def spread(block, kv, zs, dp_count, ident):
    own, width = block.shape
    ys, xs = 2, dp_count // 4
    bf = jnp.bfloat16
    dma = pltpu.SemaphoreType.DMA
    vmem, hbm = pl.BlockSpec(memory_space=pltpu.VMEM), pl.BlockSpec(memory_space=pl.ANY)
    outs = [jax.ShapeDtypeStruct((zs, ys, xs, 2, own, width), bf)]
    scratch = [dma((1,)), dma((2, zs)), dma((2, zs, ys, xs, ys + xs - 1)), dma((2, zs, ys, xs, 2))]
    args = [block]
    if kv is not None:
        args.append(kv)
        outs.append(jax.ShapeDtypeStruct((zs,) + kv.shape, bf))
        scratch += [dma((1,)), dma((zs,)), dma((zs,))]
    out = pl.pallas_call(
        functools.partial(spread_kernel, zs, ys, xs, width, half_columns(width), kv is not None),
        out_shape=outs,
        in_specs=[vmem] * len(args),
        out_specs=[hbm] * len(outs),
        scratch_shapes=scratch,
        compiler_params=pltpu.CompilerParams(collective_id=ident, has_side_effects=True),
        cost_estimate=pl.CostEstimate(flops=1 << 20, bytes_accessed=24 << 20, transcendentals=0),
        name="spread",
    )(*args)
    return out[0].reshape(-1, own, width), (out[1] if kv is not None else None)


def fold_kernel(zs, ys, xs, width, cut, with_kv, *refs):
    refs = list(refs)
    term = refs.pop(0)
    kv_ref = refs.pop(0) if with_kv else None
    out_ref = refs.pop(0)
    kv_out = refs.pop(0) if with_kv else None
    (crecv, s1, r2a, s2a, r3a, s3a, r4a, r2b, s2b, r3b, s3b, r4b, c_s, c_r) = refs[:14]
    (a2_s, a2_r, a3_s, a3_r, a4_s, a4_r, b2_s, b2_r, b3_s, b3_r, b4_s, b4_r) = refs[14:26]
    kv_got, kv_s, kv_r = refs[26:29] if with_kv else (None, None, None)
    z = lax.axis_index("seq")
    d = lax.axis_index("dp")
    y, x, c = d // (2 * xs), (d // 2) % xs, d % 2
    left, right = pl.ds(0, cut), pl.ds(cut, width - cut)
    f32, bf = jnp.float32, jnp.bfloat16

    def dev(zz, yy, xx, cc):
        return (zz, (yy * xs + xx) * 2 + cc)

    barrier = pltpu.get_barrier_semaphore()
    near = [dev(flip(z, dz, zs), y, x, c) for dz in range(1, zs)]
    near += [dev(z, (y + dy) % ys, x, c) for dy in range(1, ys)]
    near += [dev(z, y, (x + dx) % xs, c) for dx in range(1, xs)]
    near += [dev(z, y, x, 1 - c)]
    for peer in near:
        pl.semaphore_signal(barrier, inc=1, device_id=peer, device_id_type=MESH)
    pl.semaphore_wait(barrier, len(near))

    def remote(src, dst, send, recv, to):
        return pltpu.make_async_remote_copy(
            src_ref=src, dst_ref=dst, send_sem=send, recv_sem=recv, device_id=to, device_id_type=MESH
        )

    def core_copy(zz, yy, xx):
        return remote(
            term.at[zz, yy, xx, 1 - c], crecv.at[zz, yy, xx], c_s.at[zz, yy, xx], c_r.at[zz, yy, xx], dev(z, y, x, 1 - c)
        )

    def kv_copy(dz):
        zz = flip(z, dz, zs)
        return remote(kv_ref.at[zz], kv_got.at[dz], kv_s.at[dz], kv_r.at[dz], dev(zz, y, x, c))

    def a2(zz, yy, dx):
        to = dev(z, y, (x + dx) % xs, c)
        src = s1.at[zz, yy, (x + dx) % xs, :, left]
        return remote(src, r2a.at[xs - dx - 1, zz, yy], a2_s.at[dx - 1, zz, yy], a2_r.at[xs - dx - 1, zz, yy], to)

    def b2(zz, xx, dy):
        to = dev(z, (y + dy) % ys, x, c)
        src = s1.at[zz, (y + dy) % ys, xx, :, right]
        return remote(src, r2b.at[ys - dy - 1, zz, xx], b2_s.at[dy - 1, zz, xx], b2_r.at[ys - dy - 1, zz, xx], to)

    def a3(zz, dy):
        to = dev(z, (y + dy) % ys, x, c)
        src = s2a.at[zz, (y + dy) % ys]
        return remote(src, r3a.at[ys - dy - 1, zz], a3_s.at[dy - 1, zz], a3_r.at[ys - dy - 1, zz], to)

    def b3(zz, dx):
        to = dev(z, y, (x + dx) % xs, c)
        src = s2b.at[zz, (x + dx) % xs]
        return remote(src, r3b.at[xs - dx - 1, zz], b3_s.at[dx - 1, zz], b3_r.at[xs - dx - 1, zz], to)

    def a4(dz):
        zz = flip(z, dz, zs)
        return remote(s3a.at[dz], r4a.at[dz], a4_s.at[dz], a4_r.at[dz], dev(zz, y, x, c))

    def b4(dz):
        zz = flip(z, dz, zs)
        return remote(s3b.at[dz], r4b.at[dz], b4_s.at[dz], b4_r.at[dz], dev(zz, y, x, c))

    if with_kv:
        for dz in range(1, zs):
            kv_copy(dz).start()

    def first(t, carry):
        zz = flip(z, zs - 1 - t, zs)
        for yy in range(ys):
            for xx in range(xs):
                core_copy(zz, yy, xx).start()
        return carry

    lax.fori_loop(0, zs, first, 0)

    def step(t, carry):
        @pl.when(t < zs)
        def _():
            zz = flip(z, zs - 1 - t, zs)
            for yy in range(ys):
                for xx in range(xs):
                    core_copy(zz, yy, xx).wait_recv()
                    total = term[zz, yy, xx, c].astype(f32) + crecv[zz, yy, xx].astype(f32)
                    s1[zz, yy, xx] = total.astype(bf)
            for dx in range(1, xs):
                for yy in range(ys):
                    a2(zz, yy, dx).start()
            for dy in range(1, ys):
                for xx in range(xs):
                    b2(zz, xx, dy).start()

        @pl.when(jnp.logical_and(t >= 1, t < zs + 1))
        def _():
            zz = flip(z, zs - t, zs)
            for yy in range(ys):
                total = s1[zz, yy, x, :, left].astype(f32)
                for dx in range(1, xs):
                    a2(zz, yy, dx).wait_recv()
                    total = total + r2a[xs - dx - 1, zz, yy].astype(f32)
                s2a[zz, yy] = total.astype(bf)
            for dy in range(1, ys):
                a3(zz, dy).start()
            for xx in range(xs):
                total = s1[zz, y, xx, :, right].astype(f32)
                for dy in range(1, ys):
                    b2(zz, xx, dy).wait_recv()
                    total = total + r2b[ys - dy - 1, zz, xx].astype(f32)
                s2b[zz, xx] = total.astype(bf)
            for dx in range(1, xs):
                b3(zz, dx).start()

        @pl.when(t >= 2)
        def _():
            dz = zs + 1 - t
            zz = flip(z, dz, zs)
            total = s2a[zz, y].astype(f32)
            for dy in range(1, ys):
                a3(zz, dy).wait_recv()
                total = total + r3a[ys - dy - 1, zz].astype(f32)
            other = s2b[zz, x].astype(f32)
            for dx in range(1, xs):
                b3(zz, dx).wait_recv()
                other = other + r3b[xs - dx - 1, zz].astype(f32)

            @pl.when(dz > 0)
            def _():
                s3a[dz] = total.astype(bf)
                a4(dz).start()
                s3b[dz] = other.astype(bf)
                b4(dz).start()

            @pl.when(dz == 0)
            def _():
                out_ref[:, left] = total
                out_ref[:, right] = other

        return carry

    lax.fori_loop(0, zs + 2, step, 0)
    total = out_ref[:, left]
    other = out_ref[:, right]
    for dz in range(1, zs):
        a4(dz).wait_recv()
        total = total + r4a[dz].astype(f32)
        b4(dz).wait_recv()
        other = other + r4b[dz].astype(f32)
    out_ref[:, left] = total
    out_ref[:, right] = other
    if with_kv:
        kv_total = kv_ref[z].astype(f32)
        for dz in range(1, zs):
            kv_copy(dz).wait_recv()
            kv_total = kv_total + kv_got[dz].astype(f32)
        kv_out[...] = kv_total
        for dz in range(1, zs):
            kv_copy(dz).wait_send()

    def settle(zz, carry):
        for yy in range(ys):
            for xx in range(xs):
                core_copy(zz, yy, xx).wait_send()
        for dx in range(1, xs):
            for yy in range(ys):
                a2(zz, yy, dx).wait_send()
            b3(zz, dx).wait_send()
        for dy in range(1, ys):
            for xx in range(xs):
                b2(zz, xx, dy).wait_send()
            a3(zz, dy).wait_send()
        return carry

    lax.fori_loop(0, zs, settle, 0)
    for dz in range(1, zs):
        a4(dz).wait_send()
        b4(dz).wait_send()


def fold(term, kv, zs, dp_count, ident):
    own, width = term.shape[1:]
    ys, xs = 2, dp_count // 4
    cut = half_columns(width)
    rest = width - cut
    bf, f32 = jnp.bfloat16, jnp.float32
    dma = pltpu.SemaphoreType.DMA
    vmem = pl.BlockSpec(memory_space=pltpu.VMEM)
    outs = [jax.ShapeDtypeStruct((own, width), f32)]
    args = [term.reshape(zs, ys, xs, 2, own, width)]
    sizes = [
        (zs, ys, xs, own, width),
        (zs, ys, xs, own, width),
        (xs - 1, zs, ys, own, cut),
        (zs, ys, own, cut),
        (ys - 1, zs, own, cut),
        (zs, own, cut),
        (zs, own, cut),
        (ys - 1, zs, xs, own, rest),
        (zs, xs, own, rest),
        (xs - 1, zs, own, rest),
        (zs, own, rest),
        (zs, own, rest),
    ]
    scratch = [pltpu.VMEM(size, bf) for size in sizes]
    scratch += [dma((zs, ys, xs))] * 2
    scratch += [dma((xs - 1, zs, ys))] * 2 + [dma((ys - 1, zs))] * 2 + [dma((zs,))] * 2
    scratch += [dma((ys - 1, zs, xs))] * 2 + [dma((xs - 1, zs))] * 2 + [dma((zs,))] * 2
    if kv is not None:
        args.append(kv)
        outs.append(jax.ShapeDtypeStruct(kv.shape[1:], f32))
        scratch += [pltpu.VMEM(kv.shape, bf), dma((zs,)), dma((zs,))]
    out = pl.pallas_call(
        functools.partial(fold_kernel, zs, ys, xs, width, cut, kv is not None),
        out_shape=outs,
        in_specs=[vmem] * len(args),
        out_specs=[vmem] * len(outs),
        scratch_shapes=scratch,
        compiler_params=pltpu.CompilerParams(collective_id=ident, has_side_effects=True),
        cost_estimate=pl.CostEstimate(flops=1 << 20, bytes_accessed=24 << 20, transcendentals=0),
        name="fold",
    )(*args)
    return out[0], (out[1] if kv is not None else None)


def local(
    stream,
    stream_grad,
    lengths,
    w_qkv,
    w_out,
    w_gate,
    w_up,
    w_down,
    g_attn_in,
    g_query,
    g_key,
    g_attn_out,
    g_ffn_in,
    g_ffn_out,
):
    rows_in = stream[0]
    rows_grad = stream_grad[0]
    lens = lengths[0]
    rows = rows_in.shape[0]
    width = rows_in.shape[1]
    qwidth = HEADS * HEAD_DIM
    seq_count = lax.axis_size("seq")
    dp_count = lax.axis_size("dp")
    count = seq_count * dp_count
    keys = seq_count * rows
    scale = 1.0 / math.sqrt(HEAD_DIM)
    block_id = lax.axis_index("seq")
    qkv_own = w_qkv.shape[0]
    qkv_pad = (qkv_own + 8) // 8 * 8
    lane = jnp.arange(qkv_pad, dtype=jnp.int32)[None, :]
    owner = jnp.arange(count, dtype=jnp.int32)[:, None]
    qkv_origin = jnp.where(lane < qkv_own, owner * qkv_own + lane, -1).reshape(-1)
    qkv_order = one_hot_order(qkv_origin, width)
    w_qkv_pad = jnp.pad(w_qkv, ((0, qkv_pad - qkv_own), (0, 0)))
    qkv_full, _ = spread(w_qkv_pad, None, seq_count, dp_count, 2)
    qkv_full = qkv_full.reshape(count * qkv_pad, -1)
    groups = group_width(dp_count)
    ffn_rows = [(w_gate, w_up, w_down)] + [
        tuple(swapped(w, "dp", 2 * i) for w in (w_gate, w_up, w_down)) for i in range(1, groups // 2)
    ]
    starts = jnp.cumsum(lens) - lens
    own_index = block_id * rows + jnp.arange(rows, dtype=jnp.int32)
    key_index = jnp.arange(keys, dtype=jnp.int32)
    own_begin = seq_begin(own_index, starts)
    key_begin = seq_begin(key_index, starts)
    mask = (
        (key_begin[None, :] == own_begin[:, None])
        & (key_index[None, :] <= own_index[:, None])
        & (own_index[:, None] - key_index[None, :] < WINDOW)
    )
    full_mask = mask[:, None, :]
    cos_t, sin_t = rope_tables((own_index - own_begin).astype(jnp.float32), HEAD_DIM)
    root_attn = inv_root(rows_in)
    unit_attn = rows_in * root_attn
    attn_input = (unit_attn * g_attn_in).astype(jnp.bfloat16)
    attn_slots = dot32(attn_input, qkv_order).astype(jnp.bfloat16)
    projected = dot32(attn_slots, qkv_full)
    query = projected[:, :qwidth].reshape(rows, HEADS, HEAD_DIM)
    key_raw = projected[:, qwidth : qwidth + HEAD_DIM]
    value_raw = projected[:, qwidth + HEAD_DIM :]
    root_query = inv_root(query)
    unit_query = query * root_query
    query_norm = unit_query * g_query
    root_key = inv_root(key_raw)
    unit_key = key_raw * root_key
    key_norm = unit_key * g_key
    query_rot = query_norm * cos_t[:, None, :] + turn_half(query_norm) * sin_t[:, None, :]
    key_rot = key_norm * cos_t + turn_half(key_norm) * sin_t
    query_b = query_rot.astype(jnp.bfloat16)
    kv_own = jnp.concatenate([key_rot.astype(jnp.bfloat16), value_raw.astype(jnp.bfloat16)], axis=1)
    out_full, kv_all = spread(w_out, kv_own, seq_count, dp_count, 3)
    out_full = out_full.reshape(qwidth, width)
    kv_all = kv_all.reshape(keys, 2 * HEAD_DIM)
    keys_b = kv_all[:, :HEAD_DIM]
    values_b = kv_all[:, HEAD_DIM:]
    scores = jnp.einsum("rhd,kd->rhk", query_b, keys_b, preferred_element_type=jnp.float32) * scale
    logsum = jnp.log(jnp.sum(jnp.where(full_mask, jnp.exp(scores), 0.0), axis=-1))
    probs = jnp.where(full_mask, jnp.exp(scores - logsum[..., None]), 0.0)
    probs_b = probs.astype(jnp.bfloat16)
    mixed = jnp.einsum("rhk,kd->rhd", probs_b, values_b, preferred_element_type=jnp.float32)
    mixed_b = mixed.reshape(rows, qwidth).astype(jnp.bfloat16)
    attn_out = dot32(mixed_b, out_full)
    root_post = inv_root(attn_out)
    unit_post = attn_out * root_post
    hidden_in = rows_in + unit_post * g_attn_out
    root_ffn = inv_root(hidden_in)
    unit_ffn = hidden_in * root_ffn
    ffn_input = (unit_ffn * g_ffn_in).astype(jnp.bfloat16)

    result, grad_g_ffn_out, ffn_in_grad, kept, passed = ffn_block(
        ffn_input, hidden_in, rows_grad, g_ffn_out, ffn_rows, seq_count, dp_count
    )
    grad_g_ffn_out = grad_g_ffn_out[0]
    for i in range(1, groups // 2):
        kept = kept + swapped(passed[i - 1], "dp", 2 * i).astype(jnp.float32)
    grad_w_gate, grad_w_up, grad_w_down = kept[0], kept[1], kept[2]
    grad_g_ffn_in = jnp.sum(ffn_in_grad * unit_ffn, axis=0)
    hidden_grad_in = rows_grad + norm_back(ffn_in_grad, unit_ffn, root_ffn, g_ffn_in)
    grad_g_attn_out = jnp.sum(hidden_grad_in * unit_post, axis=0)
    attn_grad_b = norm_back(hidden_grad_in, unit_post, root_post, g_attn_out).astype(jnp.bfloat16)
    mixed_grad_b = contract_cols(attn_grad_b, out_full).astype(jnp.bfloat16)
    out_term = contract_rows(mixed_b, attn_grad_b).astype(jnp.bfloat16).reshape((count,) + w_out.shape)
    mixed_grad3 = mixed_grad_b.reshape(rows, HEADS, HEAD_DIM)
    delta = jnp.sum(
        mixed_grad3.astype(jnp.float32)
        * mixed_b.reshape(rows, HEADS, HEAD_DIM).astype(jnp.float32),
        axis=-1,
    )
    scores_again = (
        jnp.einsum("rhd,kd->rhk", query_b, keys_b, preferred_element_type=jnp.float32) * scale
    )
    probs_again = jnp.where(full_mask, jnp.exp(scores_again - logsum[..., None]), 0.0)
    probs_again_b = probs_again.astype(jnp.bfloat16)
    value_grad_all = jnp.einsum(
        "rhk,rhd->kd", probs_again_b, mixed_grad3, preferred_element_type=jnp.float32
    )
    prob_grad = jnp.einsum("rhd,kd->rhk", mixed_grad3, values_b, preferred_element_type=jnp.float32)
    score_grad_b = (probs_again * (prob_grad - delta[..., None])).astype(jnp.bfloat16)
    query_rot_grad = (
        jnp.einsum("rhk,kd->rhd", score_grad_b, keys_b, preferred_element_type=jnp.float32) * scale
    )
    key_grad_all = (
        jnp.einsum("rhk,rhd->kd", score_grad_b, query_b, preferred_element_type=jnp.float32) * scale
    )
    kv_grad_all = jnp.concatenate([key_grad_all, value_grad_all], axis=1)
    owned_out, kv_grad = fold(
        out_term, kv_grad_all.astype(jnp.bfloat16).reshape(seq_count, rows, -1), seq_count, dp_count, 4
    )
    key_rot_grad = kv_grad[:, :HEAD_DIM]
    value_grad = kv_grad[:, HEAD_DIM:]
    query_norm_grad = query_rot_grad * cos_t[:, None, :] - turn_half(
        query_rot_grad * sin_t[:, None, :]
    )
    key_norm_grad = key_rot_grad * cos_t - turn_half(key_rot_grad * sin_t)
    grad_g_query = jnp.sum(query_norm_grad * unit_query, axis=(0, 1))
    grad_g_key = jnp.sum(key_norm_grad * unit_key, axis=0)
    query_grad = norm_back(query_norm_grad, unit_query, root_query, g_query)
    key_grad = norm_back(key_norm_grad, unit_key, root_key, g_key)
    qkv_grad_b = jnp.concatenate(
        [query_grad.reshape(rows, qwidth), key_grad, value_grad], axis=1
    ).astype(jnp.bfloat16)
    attn_in_grad = in_order(contract_cols(qkv_grad_b, qkv_full), qkv_order)
    grad_g_attn_in = jnp.sum(attn_in_grad * unit_attn, axis=0)
    input_grad = hidden_grad_in + norm_back(attn_in_grad, unit_attn, root_attn, g_attn_in)
    gains = [grad_g_attn_in, grad_g_attn_out, grad_g_ffn_in, grad_g_ffn_out, grad_g_query, grad_g_key]
    gain_terms = jnp.concatenate([g.reshape(count, -1) for g in gains], axis=1)
    qkv_term = contract_rows(attn_slots, qkv_grad_b).astype(jnp.bfloat16).reshape(count, qkv_pad, -1)
    gain_rows = jnp.pad(gain_terms, ((0, 0), (0, w_qkv.shape[1] - gain_terms.shape[1]))).astype(jnp.bfloat16)
    qkv_term = jnp.where(
        jnp.arange(qkv_pad, dtype=jnp.int32)[None, :, None] == qkv_own, gain_rows[:, None, :], qkv_term
    )
    owned_all, _ = fold(qkv_term, None, seq_count, dp_count, 5)
    owned_qkv = owned_all[:qkv_own]
    owned = owned_all[qkv_own]
    own_width, own_head = width // count, HEAD_DIM // count
    owned_gains = [owned[i * own_width : (i + 1) * own_width] for i in range(4)]
    owned_heads = [
        owned[4 * own_width + i * own_head : 4 * own_width + (i + 1) * own_head] for i in range(2)
    ]
    return (
        result[None],
        input_grad[None],
        owned_qkv,
        owned_out,
        grad_w_gate,
        grad_w_up,
        grad_w_down,
        owned_gains[0],
        owned_heads[0],
        owned_heads[1],
        owned_gains[1],
        owned_gains[2],
        owned_gains[3],
    )


def solution(mesh):
    return jax.shard_map(
        local,
        mesh=mesh,
        in_specs=(
            P("dp", "seq", None),
            P("dp", "seq", None),
            P("dp", None),
            P(("seq", "dp"), None),
            P(("seq", "dp"), None),
            P(("seq", "dp"), None),
            P(("seq", "dp"), None),
            P(("seq", "dp"), None),
            P(),
            P(),
            P(),
            P(),
            P(),
            P(),
        ),
        out_specs=(
            P("dp", "seq", None),
            P("dp", "seq", None),
            P(("seq", "dp"), None),
            P(("seq", "dp"), None),
            P(("seq", "dp"), None),
            P(("seq", "dp"), None),
            P(("seq", "dp"), None),
            P(("seq", "dp")),
            P(("seq", "dp")),
            P(("seq", "dp")),
            P(("seq", "dp")),
            P(("seq", "dp")),
            P(("seq", "dp")),
        ),
        check_vma=False,
    )
```

time: 403 us -> 388 us (0.963); the launches traced: 397 us -> 387 us
  Pallas kernels: 0 us -> 317 us
  waiting for transfers between devices: 165 us -> 0.01 us
  starting transfers between devices: 69.8 us -> 5.79 us
  other arithmetic: 55 us -> 25.7 us
  matrix products: 51.3 us -> 23.6 us
  local copies, waits for them, and re-layouts: 39.9 us -> 13.3 us
  between operations: 16.1 us -> 1.75 us
    pallas_call x0 -> x5, Pallas kernels: none -> 317 us  [the longest x1 154 us: ffn_block(): pl.pallas_call(functools.partial(ffn_kernel, zs, ys, ws, rows, width, own...]
    ppermute x54 -> x4, waiting for transfers between devices: 165 us -> 0.01 us  [swapped(): return lax.ppermute(value, axis, [(i, i ^ bit) for i in range(length)])]
    ppermute x54 -> x4, starting transfers between devices: 69.7 us -> 5.79 us  [swapped(): return lax.ppermute(value, axis, [(i, i ^ bit) for i in range(length)])]
    concatenate x26 -> x1, other arithmetic: 19.3 us -> 0.66 us  [local(): jnp.concatenate([key_rot.astype(jnp.bfloat16), value_raw.astype(jnp.bfloa...]
    slice x33 -> x0, local copies, waits for them, and re-layouts: 17.4 us -> none  [the longest x27 9.6 us: keep_half(): other = lax.slice_in_dim(value, 1, 2, axis=at).astype(jnp.bfloat16)]
    dot_general x5 -> x4, matrix products: 17.2 us -> 7.24 us  [contract_cols(): lax.dot_general(left, right, (((1,), (1,)), ((), ())), preferred_element_...]
    add x23 -> x1, other arithmetic: 11.7 us -> 2.09 us  [local(): kept = kept + swapped(passed[i - 1], 'dp', 2 * i).astype(jnp.float32)]
    dot_general x7 -> x3, matrix products: 14.3 us -> 4.93 us  [dot32(): return jnp.dot(left, right, preferred_element_type=jnp.float32)]
  transfers between devices with their start and end apart: 56 -> 4, of which waited for: 37 -> 0; matrix products, arithmetic and copies ran while one was open for 24% -> 7% of each run, Pallas kernels for 0% -> 34%
where the time goes in v1:
time: 388 us; the launch traced here: 387 us
  Pallas kernels  317 us (82%)
  other arithmetic  25.7 us (7%)
  matrix products  23.6 us (6%)
  local copies, waits for them, and re-layouts  13.3 us (3%)
  starting transfers between devices  5.79 us (1%)
    pallas_call x1, Pallas kernels, ffn_block(): pl.pallas_call(functools.partial(ffn_kernel, zs, ys, ws, rows, width, own...  154 us
    pallas_call x2, Pallas kernels, spread(): pl.pallas_call(functools.partial(spread_kernel, zs, ys, xs, width, half_c...  83.5 us
    pallas_call x2, Pallas kernels, fold(): pl.pallas_call(functools.partial(fold_kernel, zs, ys, xs, width, cut, kv...  80 us
  transfers between devices with their start and end apart: 4, of which 0 were waited for; matrix products, arithmetic and copies ran while one was open for 7% of the time, Pallas kernels for 34%

profile of v1, /device:TPU:0, one launch (start us, length us, event | category | flops | bytes accessed | tf_op | source)
XLA Modules:
  0.0 387.1 jit_solution(10753969992216178377)
XLA Ops:
  0.7 3.0 collective-permute-start
  3.8 1.9 collective-permute-start.2
  5.9 1.2 fusion.17
  7.1 1.6 pad.9.refs_0_
  8.7 49.4 %spread.2 = bf16[4,2,2,2,40,1536]{5,4,3,2,1,0:T(8,128)(2,1)} custom-call(bf16[40,1536]{1,0:T(8,128)(2,1)} %pad.9.refs_0_), custom_call_target="tpu_custom_call" | custom-call | flops 1048576 | bytes 25165824 | tf_op jit(solution)/shard_map/spread/pallas_call | solution.py:684
  58.1 1.4 fusion.7
  59.5 2.9 fusion.46
  62.7 0.2 reduce-window_clone.1
  63.1 0.2 fusion.31
  63.3 0.8 fusion.33
  64.0 0.2 reshape.320
  64.3 0.2 multiply_reduce_fusion.11
  64.8 0.8 slice_negate_fusion.1
  65.8 1.2 fusion.41
  67.0 0.7 pad_maximum_fusion.5.refs_1_
  67.7 34.1 %spread.3 = (bf16[4,2,2,2,32,1152]{5,4,3,2,1,0:T(8,128)(2,1)}, bf16[4,128,512]{2,1,0:T(8,128)(2,1)}) custom-call(bf16[32,1152]{1,0:T(8,128)(2,1)} %refs_0_.1, bf16[128,512]{1,0:T(8,128)(2,1)} %pad_maximum_fusion.5.refs_1_), custom_call_target="tpu_custom_call" | custom-call | flops 1048576 | bytes 25165824 | tf_op jit(solution)/shard_map/spread/pallas_call | solution.py:684
  101.8 1.4 fusion.23
  103.2 1.5 select_reduce_fusion
  104.8 0.6 log_bitcast_fusion
  105.4 0.4 copy-done.55
  105.8 0.2 copy-done.49
  106.0 0.4 convolution_convert_fusion.3
  106.4 0.2 copy.82
  106.6 0.6 multiply_reduce_fusion.7
  107.2 0.3 multiply_reduce_fusion.6
  107.5 0.6 iota_compare_fusion.11
  108.1 0.6 broadcast_in_dim.84.refs_3_
  108.7 0.9 multiply_convert_fusion.1.refs_0_
  109.6 153.5 %ffn_block.1 = (f32[128,1152]{1,0:T(8,128)}, f32[1,1152]{1,0:T(1,128)}, f32[128,1152]{1,0:T(8,128)}, f32[3,216,1152]{2,1,0:T(8,128)}, bf16[1,3,216,1152]{3,2,1,0:T(8,128)(2,1)}) custom-call(bf16[128,1152]{1,0:T(8,128)(2,1)} %multiply_convert_fusion.1.refs_0_, f32[128,1152]{1,0:T(8,128)} %copy-done.2, f32[128,1152]{1,0:T(8,128)} %bitcast.146, ...), custom_call_target="tpu_custom_call" | custom-call | flops 18345885696 | bytes 41943040 | tf_op jit(solution)/shard_map/ffn_block/pallas_call | solution.py:469
  263.2 1.6 multiply_reduce_fusion
  264.8 2.2 multiply_reduce_fusion.1
  267.0 0.2 multiply_convert_fusion
  267.3 2.3 convolution_convert_fusion.1
  269.5 0.9 convolution_convert_fusion.2
  270.4 0.2 copy.83
  270.6 0.1 copy.85
  270.9 1.7 fusion.9
  272.7 0.3 fusion.11
  273.1 1.8 fusion.12
  274.9 0.8 pad_maximum_fusion.refs_1_
  275.7 30.3 %fold.2 = (f32[32,1152]{1,0:T(8,128)}, f32[128,512]{1,0:T(8,128)}) custom-call(bf16[4,2,2,2,32,1152]{5,4,3,2,1,0:T(8,128)(2,1)} %bitcast.137, bf16[4,128,512]{2,1,0:T(8,128)(2,1)} %pad_maximum_fusion.refs_1_), custom_call_target="tpu_custom_call" | custom-call | flops 1048576 | bytes 25165824 | tf_op jit(solution)/shard_map/fold/pallas_call | solution.py:913
  306.1 1.0 slice.183
  307.0 1.4 broadcast_multiply_fusion.2
  308.6 1.3 multiply_reduce_fusion.12
  309.9 1.0 multiply_convert_fusion.5
  311.0 0.3 broadcast_multiply_fusion
  311.4 0.3 multiply_reduce_fusion.8
  311.7 0.2 multiply_convert_fusion.3
  311.9 0.2 copy.86
  312.1 3.5 fusion.37
  315.7 3.1 convolution_convert_fusion
  318.8 1.3 fusion
  320.1 1.5 multiply_reduce_fusion.2
  322.5 0.7 collective-permute-start.3
  323.3 4.3 %broadcast_select_fusion.refs_0_ = bf16[4,2,2,2,40,1536]{5,4,3,2,1,0:T(8,128)(2,1)} fusion(bf16[4,2,2,2,40,1536]{5,4,3,2,1,0:T(8,128)(2,1)} %bitcast.130, pred[40]{0:T(512)(128)(4,1)S(1)} %copy-done.53, bf16[4,2,2,2,1536]{4,3,2,1,0:T(2,128)(2,1)S(1)} %broadcast_in_dim.146), kind=kLoop, calls=%fused_computation.5 | loop fusion | flops 1966080 | bytes 7962664 | tf_op jit(solution)/shard_map/jit(_where)/select_n | solution.py:1075
  327.6 49.8 %fold.3 = f32[40,1536]{1,0:T(8,128)} custom-call(bf16[4,2,2,2,40,1536]{5,4,3,2,1,0:T(8,128)(2,1)} %broadcast_select_fusion.refs_0_), custom_call_target="tpu_custom_call" | custom-call | flops 1048576 | bytes 25165824 | tf_op jit(solution)/shard_map/fold/pallas_call | solution.py:913
  377.4 1.3 slice_bitcast_fusion.12
  378.7 1.4 slice_bitcast_fusion.9
  380.1 1.0 add_bitcast_fusion
  381.2 2.1 convert_add_fusion
  383.3 1.7 slice_bitcast_fusion
  384.9 0.8 copy.117
  385.8 0.7 copy.118
  386.5 0.7 copy.119
  (157 shorter events, 2.6 us)
Async XLA Ops:
  0.6 57.4 %copy-start.7 = (f32[1,128,1152]{2,1,0:T(8,128)S(1)}, f32[1,128,1152]{2,1,0:T(8,128)}, u32[]{:S(2)}) copy-start(f32[1,128,1152]{2,1,0:T(8,128)} %param.14) | copy-start | bytes 1769476
  0.7 57.4 %copy-start.37 = (f32[1152]{0:T(1024)S(1)}, f32[1152]{0:T(1024)}, u32[]{:S(2)}) copy-start(f32[1152]{0:T(1024)} %param.22) | copy-start | bytes 13828
  0.7 108.9 %collective-permute-start = (bf16[216,1152]{1,0:T(8,128)(2,1)}, bf16[216,1152]{1,0:T(8,128)(2,1)}, u32[]{:S(2)}, u32[]{:S(2)}) collective-permute-start(bf16[216,1152]{1,0:T(8,128)(2,1)} %refs_4_.1), channel_id=1, source_target_pairs={{0,2},{1,3},{2,0},{3,1},{4,6},{5,7},{6,4},{7,5},{8,10},{9,11},{10,... | collective-permute-start | bytes 1493000 | tf_op jit(solution)/shard_map/ppermute | solution.py:33
  3.7 105.9 %collective-permute-start.1 = (bf16[216,1152]{1,0:T(8,128)(2,1)}, bf16[216,1152]{1,0:T(8,128)(2,1)}, u32[]{:S(2)}, u32[]{:S(2)}) collective-permute-start(bf16[216,1152]{1,0:T(8,128)(2,1)} %refs_5_.1), channel_id=1, source_target_pairs={{0,2},{1,3},{2,0},{3,1},{4,6},{5,7},{6,4},{7,5},{8,10},{9,11},{10,... | collective-permute-start | bytes 1493000 | tf_op jit(solution)/shard_map/ppermute | solution.py:33
  3.8 105.8 %collective-permute-start.2 = (bf16[216,1152]{1,0:T(8,128)(2,1)}, bf16[216,1152]{1,0:T(8,128)(2,1)}, u32[]{:S(2)}, u32[]{:S(2)}) collective-permute-start(bf16[216,1152]{1,0:T(8,128)(2,1)} %refs_6_.1), channel_id=1, source_target_pairs={{0,2},{1,3},{2,0},{3,1},{4,6},{5,7},{6,4},{7,5},{8,10},{9,11},{10,... | collective-permute-start | bytes 1493000 | tf_op jit(solution)/shard_map/ppermute | solution.py:33
  5.9 53.6 %copy-start.39 = (s32[1280]{0:T(1024)}, s32[1280]{0:T(1024)S(1)}, u32[]{:S(2)}) copy-start(s32[1280]{0:T(1024)S(1)} %select_n.46) | copy-start | bytes 15364
  7.1 52.4 %copy-start.51 = (f32[128]{0:T(128)}, f32[128]{0:T(128)S(1)}, u32[]{:S(2)}) copy-start(f32[128]{0:T(128)S(1)} %add_rsqrt_fusion.4) | copy-start | bytes 1540
  59.5 3.0 copy-start.10
  59.5 3.2 copy-start.54
  59.5 5.1 %copy-start.35 = (f32[256]{0:T(256)S(1)}, f32[256]{0:T(256)}, u32[]{:S(2)}) copy-start(f32[256]{0:T(256)} %param.23) | copy-start | bytes 3076
  62.5 4.5 %copy-start.9 = (f32[128,1536]{1,0:T(8,128)}, f32[128,1536]{1,0:T(8,128)S(1)}, u32[]{:S(2)}) copy-start(f32[128,1536]{1,0:T(8,128)S(1)} %fusion.46) | copy-start | bytes 2359300
  62.5 3.1 copy-start.33
  62.5 40.7 %copy-start = (f32[128,1024]{1,0:T(8,128)}, f32[128,1024]{1,0:T(8,128)S(1)}, u32[]{:S(2)}) copy-start(f32[128,1024]{1,0:T(8,128)S(1)} %slice.133) | copy-start | bytes 1572868
  63.2 42.1 %copy-start.29 = (pred[128,512]{1,0:T(8,128)(4,1)}, pred[128,512]{1,0:T(8,128)(4,1)S(1)}, u32[]{:S(2)}) copy-start(pred[128,512]{1,0:T(8,128)(4,1)S(1)} %fusion.31) | copy-start | bytes 196612
  64.6 40.2 %copy-start.31 = (f32[128,4]{0,1:T(4,128)}, f32[128,4]{0,1:T(4,128)S(1)}, u32[]{:S(2)}) copy-start(f32[128,4]{0,1:T(4,128)S(1)} %add_rsqrt_fusion) | copy-start | bytes 6148
  65.6 37.6 %copy-start.42 = (f32[128]{0:T(128)}, f32[128]{0:T(128)S(1)}, u32[]{:S(2)}) copy-start(f32[128]{0:T(128)S(1)} %add_rsqrt_fusion.3) | copy-start | bytes 1540
  65.8 36.0 %copy-start.16 = (f32[128,128]{1,0:T(8,128)}, f32[128,128]{1,0:T(8,128)S(1)}, u32[]{:S(2)}) copy-start(f32[128,128]{1,0:T(8,128)S(1)} %get-tuple-element.78) | copy-start | bytes 196612
  101.8 4.2 %copy-start.23 = (bf16[4,128,512]{2,1,0:T(8,128)(2,1)S(1)}, bf16[4,128,512]{2,1,0:T(8,128)(2,1)}, u32[]{:S(2)}) copy-start(bf16[4,128,512]{2,1,0:T(8,128)(2,1)} %get-tuple-element.22) | copy-start | bytes 1572868
  101.8 4.8 %copy-start.5 = (bf16[4,2,2,2,32,1152]{5,4,3,2,1,0:T(8,128)(2,1)S(1)}, bf16[4,2,2,2,32,1152]{5,4,3,2,1,0:T(8,128)(2,1)}, u32[]{:S(2)}) copy-start(bf16[4,2,2,2,32,1152]{5,4,3,2,1,0:T(8,128)(2,1)} %get-tuple-element.23) | copy-start | bytes 7077892
  103.2 2.2 copy-start.20
  104.8 1.0 copy-start.55
  104.8 2.4 copy-start.26
  105.4 0.6 copy-start.49
  106.3 3.2 copy-start.14
  106.4 1.7 copy-start.41
  106.4 2.3 copy-start.25
  106.6 3.0 copy-start.12
  107.2 2.4 copy-start.3
  107.2 2.4 copy-start.44
  107.5 1.2 copy-start.2
  107.5 2.1 copy-start.46
  263.1 3.9 copy-start.4
  263.1 3.9 copy-start.27
  263.2 3.9 copy-start.45
  263.2 4.0 %copy-start.13 = (bf16[128,4,256]{0,2,1:T(8,128)(2,1)S(1)}, bf16[128,4,256]{0,2,1:T(8,128)(2,1)}, u32[]{:S(2)}) copy-start(bf16[128,4,256]{0,2,1:T(8,128)(2,1)} %copy-done.12) | copy-start | bytes 786436
  264.8 4.8 %copy-start.6 = (bf16[4,2,2,2,32,1152]{5,4,3,2,1,0:T(8,128)(2,1)S(1)}, bf16[4,2,2,2,32,1152]{5,4,3,2,1,0:T(8,128)(2,1)}, u32[]{:S(2)}) copy-start(bf16[4,2,2,2,32,1152]{5,4,3,2,1,0:T(8,128)(2,1)} %get-tuple-element.23) | copy-start | bytes 7077892
  267.2 3.5 copy-start.15
  267.2 3.7 copy-start.24
  267.2 3.7 copy-start.30
  267.2 3.7 copy-start.50
  269.5 3.2 copy-start.21
  270.4 2.6 copy-start.28
  270.4 2.6 copy-start.48
  273.1 34.0 %copy-start.17 = (f32[128,128]{1,0:T(8,128)S(1)}, f32[128,128]{1,0:T(8,128)}, u32[]{:S(2)}) copy-start(f32[128,128]{1,0:T(8,128)} %copy-done.16) | copy-start | bytes 196612
  274.9 33.7 %copy-start.34 = (f32[256]{0:T(256)S(1)}, f32[256]{0:T(256)}, u32[]{:S(2)}) copy-start(f32[256]{0:T(256)} %param.24) | copy-start | bytes 3076
  274.9 33.7 %copy-start.43 = (f32[128]{0:T(128)S(1)}, f32[128]{0:T(128)}, u32[]{:S(2)}) copy-start(f32[128]{0:T(128)} %copy-done.42) | copy-start | bytes 1540
  306.0 5.4 %copy-start.1 = (f32[128,1024]{1,0:T(8,128)S(1)}, f32[128,1024]{1,0:T(8,128)}, u32[]{:S(2)}) copy-start(f32[128,1024]{1,0:T(8,128)} %copy-done) | copy-start | bytes 1572868
  306.0 5.4 %copy-start.32 = (f32[128,4]{0,1:T(4,128)S(1)}, f32[128,4]{0,1:T(4,128)}, u32[]{:S(2)}) copy-start(f32[128,4]{0,1:T(4,128)} %copy-done.31) | copy-start | bytes 6148
  306.0 5.4 %copy-start.36 = (f32[256]{0:T(256)S(1)}, f32[256]{0:T(256)}, u32[]{:S(2)}) copy-start(f32[256]{0:T(256)} %param.23) | copy-start | bytes 3076
  311.9 3.7 copy-start.11
  315.7 3.1 copy-start.40
  315.7 4.4 %copy-start.8 = (f32[1,128,1152]{2,1,0:T(8,128)S(1)}, f32[1,128,1152]{2,1,0:T(8,128)}, u32[]{:S(2)}) copy-start(f32[1,128,1152]{2,1,0:T(8,128)} %param.14) | copy-start | bytes 1769476
  315.7 4.4 %copy-start.38 = (f32[1152]{0:T(1024)S(1)}, f32[1152]{0:T(1024)}, u32[]{:S(2)}) copy-start(f32[1152]{0:T(1024)} %param.22) | copy-start | bytes 13828
  315.7 4.4 %copy-start.52 = (f32[128]{0:T(128)S(1)}, f32[128]{0:T(128)}, u32[]{:S(2)}) copy-start(f32[128]{0:T(128)} %copy-done.51) | copy-start | bytes 1540
  318.8 3.2 copy-start.47
  318.8 4.5 %copy-start.53 = (pred[40]{0:T(512)(128)(4,1)S(1)}, pred[40]{0:T(512)(128)(4,1)}, u32[]{:S(2)}) copy-start(pred[40]{0:T(512)(128)(4,1)} %iota_compare_fusion.11) | copy-start | bytes 124
  322.5 58.6 %collective-permute-start.3 = (bf16[3,216,1152]{2,1,0:T(8,128)(2,1)}, bf16[3,216,1152]{2,1,0:T(8,128)(2,1)S(1)}, u32[]{:S(2)}, u32[]{:S(2)}) collective-permute-start(bf16[3,216,1152]{2,1,0:T(8,128)(2,1)} %bitcast.153), channel_id=1, source_target_pairs={{0,2},{1,3},{2,0},{3,1},{4,6},{5,7},{6,4},{7,5},{8,10},{9,11},{10,... | collective-permute-start | bytes 4478984 | tf_op jit(solution)/shard_map/ppermute | solution.py:33
  383.2 1.7 copy-start.19
  383.3 2.5 copy-start.18
  383.3 3.2 copy-start.22

commit v2 on v1

--- a/solution.py
+++ b/solution.py
@@ -26,11 +26,6 @@
         bits.append(bit)
         bit *= 2
     return bits
-
-
-def swapped(value, axis, bit):
-    length = lax.axis_size(axis)
-    return lax.ppermute(value, axis, [(i, i ^ bit) for i in range(length)])
 
 
 def one_hot_order(origin, count):
@@ -482,18 +477,10 @@
     return out[0], out[1], out[2], out[3], passed
 
 
-def spread_kernel(zs, ys, xs, width, cut, with_kv, *refs):
-    refs = list(refs)
-    w_ref = refs.pop(0)
-    kv_ref = refs.pop(0) if with_kv else None
-    out_ref = refs.pop(0)
-    kv_out = refs.pop(0) if with_kv else None
-    own_s, z_s, far_s, far_r = refs[:4]
-    kv_own, kv_s, kv_r = refs[4:7] if with_kv else (None, None, None)
+def neighbours(zs, ys, xs):
     z = lax.axis_index("seq")
     d = lax.axis_index("dp")
     y, x, c = d // (2 * xs), (d // 2) % xs, d % 2
-    cols = (pl.ds(0, cut), pl.ds(cut, width - cut))
 
     def dev(zz, yy, xx, cc):
         return (zz, (yy * xs + xx) * 2 + cc)
@@ -501,230 +488,188 @@
     barrier = pltpu.get_barrier_semaphore()
     near = [dev(flip(z, dz, zs), y, x, c) for dz in range(1, zs)]
     near += [dev(z, (y + dy) % ys, x, c) for dy in range(1, ys)]
-    near += [dev(z, y, (x + dx) % xs, c) for dx in range(1, xs)]
+    near += [dev(z, y, flip(x, dx, xs), c) for dx in range(1, xs)]
     near += [dev(z, y, x, 1 - c)]
     for peer in near:
         pl.semaphore_signal(barrier, inc=1, device_id=peer, device_id_type=MESH)
     pl.semaphore_wait(barrier, len(near))
-
-    def slot(h, zz, yy, xx, cc):
-        return out_ref.at[zz, yy, xx, cc, :, cols[h]]
-
-    def copy(h, src, zz, yy, xx, send, to):
-        return pltpu.make_async_remote_copy(
-            src_ref=src,
-            dst_ref=slot(h, zz, yy, xx, c),
-            send_sem=send,
-            recv_sem=far_r.at[h, zz, yy, xx, c],
-            device_id=to,
-            device_id_type=MESH,
-        )
-
-    def along(h, dz):
-        return copy(h, w_ref.at[:, cols[h]], z, y, x, z_s.at[h, dz], dev(flip(z, dz, zs), y, x, c))
-
-    def over_y(h, src, zz, yy, xx, dy):
-        return copy(h, src, zz, yy, xx, far_s.at[h, zz, yy, xx, dy], dev(z, (y + dy) % ys, x, c))
-
-    def over_x(h, src, zz, yy, xx, dx):
-        return copy(h, src, zz, yy, xx, far_s.at[h, zz, yy, xx, ys - 1 + dx], dev(z, y, (x + dx) % xs, c))
-
-    def over_core(h, src, zz, yy, xx):
-        return copy(h, src, zz, yy, xx, far_s.at[h, zz, yy, xx, 0], dev(z, y, x, 1 - c))
-
-    def arrived(h, zz, yy, xx, cc):
-        pltpu.make_async_remote_copy(
-            src_ref=slot(h, zz, yy, xx, cc),
-            dst_ref=slot(h, zz, yy, xx, cc),
-            send_sem=z_s.at[h, 0],
-            recv_sem=far_r.at[h, zz, yy, xx, cc],
-            device_id=dev(z, y, x, 1 - c),
-            device_id_type=MESH,
-        ).wait_recv()
+    return z, y, x, c, dev
+
+
+def remote(src, dst, send, recv, to):
+    return pltpu.make_async_remote_copy(
+        src_ref=src, dst_ref=dst, send_sem=send, recv_sem=recv, device_id=to, device_id_type=MESH
+    )
+
+
+def spread_kernel(zs, ys, xs, with_kv, extras, *refs):
+    refs = list(refs)
+    w_ref = refs.pop(0)
+    kv_ref = refs.pop(0) if with_kv else None
+    extra_in = [refs.pop(0) for _ in range(extras)]
+    out_ref = refs.pop(0)
+    kv_out = refs.pop(0) if with_kv else None
+    extra_out = [refs.pop(0) for _ in range(extras)]
+    own_s, x_s, z_s, y_s, c_s, r, e_s, e_r = refs[:8]
+    kv_own, kv_s, kv_r = refs[8:11] if with_kv else (None, None, None)
+    z, y, x, c, dev = neighbours(zs, ys, xs)
+
+    def slot(zz, yy, xx, cc):
+        return out_ref.at[zz, yy, xx, cc]
+
+    def copy(src, zz, yy, xx, send, to):
+        return remote(src, slot(zz, yy, xx, c), send, r.at[zz, yy, xx, c], to)
+
+    def over_x(dx):
+        return copy(w_ref, z, y, x, x_s.at[dx], dev(z, y, flip(x, dx, xs), c))
+
+    def over_z(src, dx, dz):
+        return copy(src, z, y, flip(x, dx, xs), z_s.at[dx, dz], dev(flip(z, dz, zs), y, x, c))
+
+    def over_y(src, zz, dx, dy):
+        return copy(src, zz, y, flip(x, dx, xs), y_s.at[zz, dx, dy], dev(z, (y + dy) % ys, x, c))
+
+    def over_core(src, zz, yy, xx):
+        return copy(src, zz, yy, xx, c_s.at[zz, yy, xx], dev(z, y, x, 1 - c))
+
+    def arrived(zz, yy, xx, cc):
+        remote(slot(zz, yy, xx, cc), slot(zz, yy, xx, cc), x_s.at[0], r.at[zz, yy, xx, cc], dev(z, y, x, 1 - c)).wait_recv()
+
+    def extra(e, dx):
+        return remote(
+            extra_in[e], extra_out[e].at[dx - 1], e_s.at[e, dx], e_r.at[e, dx], dev(z, y, flip(x, dx, xs), c)
+        )
 
     def kv_copy(dz):
-        return pltpu.make_async_remote_copy(
-            src_ref=kv_ref,
-            dst_ref=kv_out.at[z],
-            send_sem=kv_s.at[dz],
-            recv_sem=kv_r.at[z],
-            device_id=dev(flip(z, dz, zs), y, x, c),
-            device_id_type=MESH,
-        )
+        return remote(kv_ref, kv_out.at[z], kv_s.at[dz], kv_r.at[z], dev(flip(z, dz, zs), y, x, c))
 
     def kv_arrived(zz):
-        pltpu.make_async_remote_copy(
-            src_ref=kv_ref,
-            dst_ref=kv_out.at[zz],
-            send_sem=kv_s.at[0],
-            recv_sem=kv_r.at[zz],
-            device_id=dev(z, y, x, 1 - c),
-            device_id_type=MESH,
-        ).wait_recv()
-
-    def onward(h, src, zz):
-        if h == 0:
-            for dy in range(1, ys):
-                over_y(h, src, zz, y, x, dy).start()
-        for dx in range(1, xs):
-            over_x(h, src, zz, y, x, dx).start()
-        if h == 1:
-            for dy in range(1, ys):
-                over_y(h, src, zz, y, x, dy).start()
-        over_core(h, src, zz, y, x).start()
-
+        remote(kv_ref, kv_out.at[zz], kv_s.at[0], kv_r.at[zz], dev(z, y, x, 1 - c)).wait_recv()
+
+    for dx in range(1, xs):
+        over_x(dx).start()
     if with_kv:
         for dz in range(1, zs):
             kv_copy(dz).start()
     for dz in range(1, zs):
-        for h in range(2):
-            along(h, dz).start()
-    for h in range(2):
-        onward(h, w_ref.at[:, cols[h]], z)
+        over_z(w_ref, 0, dz).start()
+    for dy in range(1, ys):
+        over_y(w_ref, z, 0, dy).start()
+    over_core(w_ref, z, y, x).start()
+    for e in range(extras):
+        for dx in range(1, xs):
+            extra(e, dx).start()
     keep = pltpu.make_async_copy(w_ref, out_ref.at[z, y, x, c], own_s.at[0])
     keep.start()
     if with_kv:
         kv_keep = pltpu.make_async_copy(kv_ref, kv_out.at[z], kv_own.at[0])
         kv_keep.start()
+    for dx in range(1, xs):
+        xx = flip(x, dx, xs)
+        arrived(z, y, xx, c)
+        src = slot(z, y, xx, c)
+        for dz in range(1, zs):
+            over_z(src, dx, dz).start()
+        for dy in range(1, ys):
+            over_y(src, z, dx, dy).start()
+        over_core(src, z, y, xx).start()
 
     def step(t, carry):
         @pl.when(t < zs)
         def _():
             zz = flip(z, t, zs)
-            for h in range(2):
-
-                @pl.when(t > 0)
-                def _():
-                    arrived(h, zz, y, x, c)
-                    onward(h, slot(h, zz, y, x, c), zz)
-
-        @pl.when(jnp.logical_and(t >= 1, t < zs + 1))
-        def _():
-            zz = flip(z, t - 1, zs)
+            for dx in range(xs):
+                xx = flip(x, dx, xs)
+                arrived(zz, y, xx, c)
+                src = slot(zz, y, xx, c)
+                for dy in range(1, ys):
+                    over_y(src, zz, dx, dy).start()
+                over_core(src, zz, y, xx).start()
+
+        zz = flip(z, t - 1, zs)
+        for dx in range(xs):
+            xx = flip(x, dx, xs)
             for dy in range(1, ys):
                 yy = (y + dy) % ys
-                arrived(0, zz, yy, x, c)
-                for dx in range(1, xs):
-                    over_x(0, slot(0, zz, yy, x, c), zz, yy, x, dx).start()
-                over_core(0, slot(0, zz, yy, x, c), zz, yy, x).start()
-            for dx in range(1, xs):
-                xx = (x + dx) % xs
-                arrived(1, zz, y, xx, c)
-                for dy in range(1, ys):
-                    over_y(1, slot(1, zz, y, xx, c), zz, y, xx, dy).start()
-                over_core(1, slot(1, zz, y, xx, c), zz, y, xx).start()
-
-        @pl.when(t >= 2)
-        def _():
-            zz = flip(z, t - 2, zs)
-            for dx in range(1, xs):
-                xx = (x + dx) % xs
-                for dy in range(ys):
-                    yy = (y + dy) % ys
-                    arrived(0, zz, yy, xx, c)
-                    over_core(0, slot(0, zz, yy, xx, c), zz, yy, xx).start()
-            for dy in range(1, ys):
-                yy = (y + dy) % ys
-                for dx in range(xs):
-                    xx = (x + dx) % xs
-                    arrived(1, zz, yy, xx, c)
-                    over_core(1, slot(1, zz, yy, xx, c), zz, yy, xx).start()
-
+                arrived(zz, yy, xx, c)
+                over_core(slot(zz, yy, xx, c), zz, yy, xx).start()
         return carry
 
-    lax.fori_loop(0, zs + 2, step, 0)
+    lax.fori_loop(1, zs + 1, step, 0)
 
     def settle(zz, carry):
         for yy in range(ys):
             for xx in range(xs):
-                for h in range(2):
-                    arrived(h, zz, yy, xx, 1 - c)
-                    over_core(h, slot(h, zz, yy, xx, c), zz, yy, xx).wait_send()
-        for dx in range(1, xs):
-            for dy in range(ys):
-                yy = (y + dy) % ys
-                over_x(0, slot(0, zz, yy, x, c), zz, yy, x, dx).wait_send()
-            over_x(1, slot(1, zz, y, x, c), zz, y, x, dx).wait_send()
-        for dy in range(1, ys):
-            for dx in range(xs):
-                xx = (x + dx) % xs
-                over_y(1, slot(1, zz, y, xx, c), zz, y, xx, dy).wait_send()
-            over_y(0, slot(0, zz, y, x, c), zz, y, x, dy).wait_send()
+                arrived(zz, yy, xx, 1 - c)
+                over_core(slot(zz, yy, xx, c), zz, yy, xx).wait_send()
+        for dx in range(xs):
+            for dy in range(1, ys):
+                over_y(slot(zz, y, x, c), zz, dx, dy).wait_send()
         return carry
 
     lax.fori_loop(0, zs, settle, 0)
     keep.wait()
+    for dx in range(1, xs):
+        over_x(dx).wait_send()
     for dz in range(1, zs):
-        for h in range(2):
-            along(h, dz).wait_send()
+        for dx in range(xs):
+            over_z(w_ref, dx, dz).wait_send()
     if with_kv:
         kv_keep.wait()
         for dz in range(1, zs):
             kv_arrived(flip(z, dz, zs))
             kv_copy(dz).wait_send()
-
-
-def half_columns(width):
-    return (width // 256) * 128 + (128 if width % 256 else 0)
-
-
-def spread(block, kv, zs, dp_count, ident):
+    for e in range(extras):
+        for dx in range(1, xs):
+            extra(e, dx).wait()
+
+
+def spread(block, kv, extra, zs, dp_count, ident):
     own, width = block.shape
     ys, xs = 2, dp_count // 4
     bf = jnp.bfloat16
     dma = pltpu.SemaphoreType.DMA
     vmem, hbm = pl.BlockSpec(memory_space=pltpu.VMEM), pl.BlockSpec(memory_space=pl.ANY)
     outs = [jax.ShapeDtypeStruct((zs, ys, xs, 2, own, width), bf)]
-    scratch = [dma((1,)), dma((2, zs)), dma((2, zs, ys, xs, ys + xs - 1)), dma((2, zs, ys, xs, 2))]
-    args = [block]
+    scratch = [dma((1,)), dma((xs,)), dma((xs, zs)), dma((zs, xs, ys)), dma((zs, ys, xs)), dma((zs, ys, xs, 2))]
+    scratch += [dma((len(extra), xs))] * 2
+    args, specs = [block], [vmem]
     if kv is not None:
         args.append(kv)
+        specs.append(vmem)
         outs.append(jax.ShapeDtypeStruct((zs,) + kv.shape, bf))
         scratch += [dma((1,)), dma((zs,)), dma((zs,))]
+    for e in extra:
+        args.append(e)
+        specs.append(hbm)
+        outs.append(jax.ShapeDtypeStruct((xs - 1,) + e.shape, bf))
     out = pl.pallas_call(
-        functools.partial(spread_kernel, zs, ys, xs, width, half_columns(width), kv is not None),
+        functools.partial(spread_kernel, zs, ys, xs, kv is not None, len(extra)),
         out_shape=outs,
-        in_specs=[vmem] * len(args),
+        in_specs=specs,
         out_specs=[hbm] * len(outs),
         scratch_shapes=scratch,
         compiler_params=pltpu.CompilerParams(collective_id=ident, has_side_effects=True),
         cost_estimate=pl.CostEstimate(flops=1 << 20, bytes_accessed=24 << 20, transcendentals=0),
         name="spread",
     )(*args)
-    return out[0].reshape(-1, own, width), (out[1] if kv is not None else None)
-
-
-def fold_kernel(zs, ys, xs, width, cut, with_kv, *refs):
+    return out[0].reshape(-1, own, width), (out[1] if kv is not None else None), out[len(out) - len(extra) :]
+
+
+def fold_kernel(zs, ys, xs, with_kv, parts, *refs):
     refs = list(refs)
     term = refs.pop(0)
     kv_ref = refs.pop(0) if with_kv else None
+    passed = refs.pop(0) if parts else None
     out_ref = refs.pop(0)
     kv_out = refs.pop(0) if with_kv else None
-    (crecv, s1, r2a, s2a, r3a, s3a, r4a, r2b, s2b, r3b, s3b, r4b, c_s, c_r) = refs[:14]
-    (a2_s, a2_r, a3_s, a3_r, a4_s, a4_r, b2_s, b2_r, b3_s, b3_r, b4_s, b4_r) = refs[14:26]
-    kv_got, kv_s, kv_r = refs[26:29] if with_kv else (None, None, None)
-    z = lax.axis_index("seq")
-    d = lax.axis_index("dp")
-    y, x, c = d // (2 * xs), (d // 2) % xs, d % 2
-    left, right = pl.ds(0, cut), pl.ds(cut, width - cut)
+    got = refs.pop(0) if parts else None
+    (crecv, s1, r2, s2, r3, s3, r4, c_s, c_r, y_s, y_r, z_s, z_r, x_s, x_r) = refs[:15]
+    refs = refs[15:]
+    e_s, e_r = (refs.pop(0), refs.pop(0)) if parts else (None, None)
+    kv_got, kv_s, kv_r = refs if with_kv else (None, None, None)
     f32, bf = jnp.float32, jnp.bfloat16
-
-    def dev(zz, yy, xx, cc):
-        return (zz, (yy * xs + xx) * 2 + cc)
-
-    barrier = pltpu.get_barrier_semaphore()
-    near = [dev(flip(z, dz, zs), y, x, c) for dz in range(1, zs)]
-    near += [dev(z, (y + dy) % ys, x, c) for dy in range(1, ys)]
-    near += [dev(z, y, (x + dx) % xs, c) for dx in range(1, xs)]
-    near += [dev(z, y, x, 1 - c)]
-    for peer in near:
-        pl.semaphore_signal(barrier, inc=1, device_id=peer, device_id_type=MESH)
-    pl.semaphore_wait(barrier, len(near))
-
-    def remote(src, dst, send, recv, to):
-        return pltpu.make_async_remote_copy(
-            src_ref=src, dst_ref=dst, send_sem=send, recv_sem=recv, device_id=to, device_id_type=MESH
-        )
+    z, y, x, c, dev = neighbours(zs, ys, xs)
 
     def core_copy(zz, yy, xx):
         return remote(
@@ -735,33 +680,25 @@
         zz = flip(z, dz, zs)
         return remote(kv_ref.at[zz], kv_got.at[dz], kv_s.at[dz], kv_r.at[dz], dev(zz, y, x, c))
 
-    def a2(zz, yy, dx):
-        to = dev(z, y, (x + dx) % xs, c)
-        src = s1.at[zz, yy, (x + dx) % xs, :, left]
-        return remote(src, r2a.at[xs - dx - 1, zz, yy], a2_s.at[dx - 1, zz, yy], a2_r.at[xs - dx - 1, zz, yy], to)
-
-    def b2(zz, xx, dy):
-        to = dev(z, (y + dy) % ys, x, c)
-        src = s1.at[zz, (y + dy) % ys, xx, :, right]
-        return remote(src, r2b.at[ys - dy - 1, zz, xx], b2_s.at[dy - 1, zz, xx], b2_r.at[ys - dy - 1, zz, xx], to)
-
-    def a3(zz, dy):
-        to = dev(z, (y + dy) % ys, x, c)
-        src = s2a.at[zz, (y + dy) % ys]
-        return remote(src, r3a.at[ys - dy - 1, zz], a3_s.at[dy - 1, zz], a3_r.at[ys - dy - 1, zz], to)
-
-    def b3(zz, dx):
-        to = dev(z, y, (x + dx) % xs, c)
-        src = s2b.at[zz, (x + dx) % xs]
-        return remote(src, r3b.at[xs - dx - 1, zz], b3_s.at[dx - 1, zz], b3_r.at[xs - dx - 1, zz], to)
-
-    def a4(dz):
-        zz = flip(z, dz, zs)
-        return remote(s3a.at[dz], r4a.at[dz], a4_s.at[dz], a4_r.at[dz], dev(zz, y, x, c))
-
-    def b4(dz):
-        zz = flip(z, dz, zs)
-        return remote(s3b.at[dz], r4b.at[dz], b4_s.at[dz], b4_r.at[dz], dev(zz, y, x, c))
+    def over_y(zz, xx, dy):
+        yy = (y + dy) % ys
+        at = ys - dy - 1
+        return remote(
+            s1.at[zz, yy, xx], r2.at[at, zz, xx], y_s.at[dy - 1, zz, xx], y_r.at[at, zz, xx], dev(z, yy, x, c)
+        )
+
+    def over_z(dz, xx):
+        return remote(
+            s2.at[dz, xx], r3.at[dz, xx], z_s.at[dz, xx], z_r.at[dz, xx], dev(flip(z, dz, zs), y, x, c)
+        )
+
+    def over_x(dx):
+        return remote(s3.at[dx], r4.at[dx], x_s.at[dx], x_r.at[dx], dev(z, y, flip(x, dx, xs), c))
+
+    def extra(k, dx):
+        return remote(
+            passed.at[dx - 1, parts[k]], got.at[dx - 1, k], e_s.at[k, dx], e_r.at[k, dx], dev(z, y, flip(x, dx, xs), c)
+        )
 
     if with_kv:
         for dz in range(1, zs):
@@ -775,80 +712,50 @@
         return carry
 
     lax.fori_loop(0, zs, first, 0)
+    for k in range(len(parts)):
+        for dx in range(1, xs):
+            extra(k, dx).start()
 
     def step(t, carry):
         @pl.when(t < zs)
         def _():
             zz = flip(z, zs - 1 - t, zs)
-            for yy in range(ys):
+            for dy in range(ys - 1, -1, -1):
+                yy = (y + dy) % ys
                 for xx in range(xs):
                     core_copy(zz, yy, xx).wait_recv()
                     total = term[zz, yy, xx, c].astype(f32) + crecv[zz, yy, xx].astype(f32)
                     s1[zz, yy, xx] = total.astype(bf)
-            for dx in range(1, xs):
-                for yy in range(ys):
-                    a2(zz, yy, dx).start()
-            for dy in range(1, ys):
-                for xx in range(xs):
-                    b2(zz, xx, dy).start()
-
-        @pl.when(jnp.logical_and(t >= 1, t < zs + 1))
+                    if dy > 0:
+                        over_y(zz, xx, dy).start()
+
+        @pl.when(t >= 1)
         def _():
-            zz = flip(z, zs - t, zs)
-            for yy in range(ys):
-                total = s1[zz, yy, x, :, left].astype(f32)
-                for dx in range(1, xs):
-                    a2(zz, yy, dx).wait_recv()
-                    total = total + r2a[xs - dx - 1, zz, yy].astype(f32)
-                s2a[zz, yy] = total.astype(bf)
-            for dy in range(1, ys):
-                a3(zz, dy).start()
+            dz = zs - t
+            zz = flip(z, dz, zs)
             for xx in range(xs):
-                total = s1[zz, y, xx, :, right].astype(f32)
+                total = s1[zz, y, xx].astype(f32)
                 for dy in range(1, ys):
-                    b2(zz, xx, dy).wait_recv()
-                    total = total + r2b[ys - dy - 1, zz, xx].astype(f32)
-                s2b[zz, xx] = total.astype(bf)
-            for dx in range(1, xs):
-                b3(zz, dx).start()
-
-        @pl.when(t >= 2)
-        def _():
-            dz = zs + 1 - t
-            zz = flip(z, dz, zs)
-            total = s2a[zz, y].astype(f32)
-            for dy in range(1, ys):
-                a3(zz, dy).wait_recv()
-                total = total + r3a[ys - dy - 1, zz].astype(f32)
-            other = s2b[zz, x].astype(f32)
-            for dx in range(1, xs):
-                b3(zz, dx).wait_recv()
-                other = other + r3b[xs - dx - 1, zz].astype(f32)
-
-            @pl.when(dz > 0)
-            def _():
-                s3a[dz] = total.astype(bf)
-                a4(dz).start()
-                s3b[dz] = other.astype(bf)
-                b4(dz).start()
-
-            @pl.when(dz == 0)
-            def _():
-                out_ref[:, left] = total
-                out_ref[:, right] = other
+                    over_y(zz, xx, dy).wait_recv()
+                    total = total + r2[ys - dy - 1, zz, xx].astype(f32)
+                s2[dz, xx] = total.astype(bf)
+
+                @pl.when(dz > 0)
+                def _():
+                    over_z(dz, xx).start()
 
         return carry
 
-    lax.fori_loop(0, zs + 2, step, 0)
-    total = out_ref[:, left]
-    other = out_ref[:, right]
-    for dz in range(1, zs):
-        a4(dz).wait_recv()
-        total = total + r4a[dz].astype(f32)
-        b4(dz).wait_recv()
-        other = other + r4b[dz].astype(f32)
-    out_ref[:, left] = total
-    out_ref[:, right] = other
+    lax.fori_loop(0, zs + 1, step, 0)
+    for dx in range(xs - 1, -1, -1):
+        xx = flip(x, dx, xs)
+        total = s2[0, xx].astype(f32)
+        for dz in range(1, zs):
+            over_z(dz, xx).wait_recv()
+            total = total + r3[dz, xx].astype(f32)
+        if dx > 0:
+            s3[dx] = total.astype(bf)
+            over_x(dx).start()
     if with_kv:
         kv_total = kv_ref[z].astype(f32)
         for dz in range(1, zs):
@@ -857,70 +764,66 @@
         kv_out[...] = kv_total
         for dz in range(1, zs):
             kv_copy(dz).wait_send()
+    for dx in range(1, xs):
+        over_x(dx).wait()
+        total = total + r4[dx].astype(f32)
+    out_ref[...] = total
 
     def settle(zz, carry):
         for yy in range(ys):
             for xx in range(xs):
                 core_copy(zz, yy, xx).wait_send()
-        for dx in range(1, xs):
-            for yy in range(ys):
-                a2(zz, yy, dx).wait_send()
-            b3(zz, dx).wait_send()
         for dy in range(1, ys):
             for xx in range(xs):
-                b2(zz, xx, dy).wait_send()
-            a3(zz, dy).wait_send()
+                over_y(zz, xx, dy).wait_send()
         return carry
 
     lax.fori_loop(0, zs, settle, 0)
     for dz in range(1, zs):
-        a4(dz).wait_send()
-        b4(dz).wait_send()
-
-
-def fold(term, kv, zs, dp_count, ident):
+        for xx in range(xs):
+            over_z(dz, xx).wait_send()
+    for k in range(len(parts)):
+        for dx in range(1, xs):
+            extra(k, dx).wait()
+
+
+def fold(term, kv, passed, parts, zs, dp_count, ident):
     own, width = term.shape[1:]
     ys, xs = 2, dp_count // 4
-    cut = half_columns(width)
-    rest = width - cut
     bf, f32 = jnp.bfloat16, jnp.float32
     dma = pltpu.SemaphoreType.DMA
-    vmem = pl.BlockSpec(memory_space=pltpu.VMEM)
-    outs = [jax.ShapeDtypeStruct((own, width), f32)]
-    args = [term.reshape(zs, ys, xs, 2, own, width)]
-    sizes = [
-        (zs, ys, xs, own, width),
-        (zs, ys, xs, own, width),
-        (xs - 1, zs, ys, own, cut),
-        (zs, ys, own, cut),
-        (ys - 1, zs, own, cut),
-        (zs, own, cut),
-        (zs, own, cut),
-        (ys - 1, zs, xs, own, rest),
-        (zs, xs, own, rest),
-        (xs - 1, zs, own, rest),
-        (zs, own, rest),
-        (zs, own, rest),
-    ]
-    scratch = [pltpu.VMEM(size, bf) for size in sizes]
-    scratch += [dma((zs, ys, xs))] * 2
-    scratch += [dma((xs - 1, zs, ys))] * 2 + [dma((ys - 1, zs))] * 2 + [dma((zs,))] * 2
-    scratch += [dma((ys - 1, zs, xs))] * 2 + [dma((xs - 1, zs))] * 2 + [dma((zs,))] * 2
+    vmem, hbm = pl.BlockSpec(memory_space=pltpu.VMEM), pl.BlockSpec(memory_space=pl.ANY)
+    outs, out_specs = [jax.ShapeDtypeStruct((own, width), f32)], [vmem]
+    args, specs = [term.reshape(zs, ys, xs, 2, own, width)], [vmem]
+    lead = [(zs, ys, xs), (zs, ys, xs), (ys - 1, zs, xs), (zs, xs), (zs, xs), (xs,), (xs,)]
+    scratch = [pltpu.VMEM(size + (own, width), bf) for size in lead]
+    scratch += [dma((zs, ys, xs))] * 2 + [dma((ys - 1, zs, xs))] * 2 + [dma((zs, xs))] * 2 + [dma((xs,))] * 2
     if kv is not None:
         args.append(kv)
+        specs.append(vmem)
         outs.append(jax.ShapeDtypeStruct(kv.shape[1:], f32))
+        out_specs.append(vmem)
+    if xs < 2:
+        parts = ()
+    if parts:
+        args.append(passed)
+        specs.append(hbm)
+        outs.append(jax.ShapeDtypeStruct((xs - 1, len(parts)) + passed.shape[2:], bf))
+        out_specs.append(hbm)
+        scratch += [dma((len(parts), xs))] * 2
+    if kv is not None:
         scratch += [pltpu.VMEM(kv.shape, bf), dma((zs,)), dma((zs,))]
     out = pl.pallas_call(
-        functools.partial(fold_kernel, zs, ys, xs, width, cut, kv is not None),
+        functools.partial(fold_kernel, zs, ys, xs, kv is not None, parts),
         out_shape=outs,
-        in_specs=[vmem] * len(args),
-        out_specs=[vmem] * len(outs),
+        in_specs=specs,
+        out_specs=out_specs,
         scratch_shapes=scratch,
         compiler_params=pltpu.CompilerParams(collective_id=ident, has_side_effects=True),
         cost_estimate=pl.CostEstimate(flops=1 << 20, bytes_accessed=24 << 20, transcendentals=0),
         name="fold",
     )(*args)
-    return out[0], (out[1] if kv is not None else None)
+    return out[0], (out[1] if kv is not None else None), (out[-1] if parts else None)
 
 
 def local(
@@ -958,12 +861,9 @@
     qkv_origin = jnp.where(lane < qkv_own, owner * qkv_own + lane, -1).reshape(-1)
     qkv_order = one_hot_order(qkv_origin, width)
     w_qkv_pad = jnp.pad(w_qkv, ((0, qkv_pad - qkv_own), (0, 0)))
-    qkv_full, _ = spread(w_qkv_pad, None, seq_count, dp_count, 2)
+    qkv_full, _, (gate_rows, up_rows) = spread(w_qkv_pad, None, [w_gate, w_up], seq_count, dp_count, 2)
     qkv_full = qkv_full.reshape(count * qkv_pad, -1)
     groups = group_width(dp_count)
-    ffn_rows = [(w_gate, w_up, w_down)] + [
-        tuple(swapped(w, "dp", 2 * i) for w in (w_gate, w_up, w_down)) for i in range(1, groups // 2)
-    ]
     starts = jnp.cumsum(lens) - lens
     own_index = block_id * rows + jnp.arange(rows, dtype=jnp.int32)
     key_index = jnp.arange(keys, dtype=jnp.int32)
@@ -994,7 +894,10 @@
     key_rot = key_norm * cos_t + turn_half(key_norm) * sin_t
     query_b = query_rot.astype(jnp.bfloat16)
     kv_own = jnp.concatenate([key_rot.astype(jnp.bfloat16), value_raw.astype(jnp.bfloat16)], axis=1)
-    out_full, kv_all = spread(w_out, kv_own, seq_count, dp_count, 3)
+    out_full, kv_all, (down_rows,) = spread(w_out, kv_own, [w_down], seq_count, dp_count, 3)
+    ffn_rows = [(w_gate, w_up, w_down)] + [
+        (gate_rows[i], up_rows[i], down_rows[i]) for i in range(groups // 2 - 1)
+    ]
     out_full = out_full.reshape(qwidth, width)
     kv_all = kv_all.reshape(keys, 2 * HEAD_DIM)
     keys_b = kv_all[:, :HEAD_DIM]
@@ -1017,9 +920,6 @@
         ffn_input, hidden_in, rows_grad, g_ffn_out, ffn_rows, seq_count, dp_count
     )
     grad_g_ffn_out = grad_g_ffn_out[0]
-    for i in range(1, groups // 2):
-        kept = kept + swapped(passed[i - 1], "dp", 2 * i).astype(jnp.float32)
-    grad_w_gate, grad_w_up, grad_w_down = kept[0], kept[1], kept[2]
     grad_g_ffn_in = jnp.sum(ffn_in_grad * unit_ffn, axis=0)
     hidden_grad_in = rows_grad + norm_back(ffn_in_grad, unit_ffn, root_ffn, g_ffn_in)
     grad_g_attn_out = jnp.sum(hidden_grad_in * unit_post, axis=0)
@@ -1049,8 +949,8 @@
         jnp.einsum("rhk,rhd->kd", score_grad_b, query_b, preferred_element_type=jnp.float32) * scale
     )
     kv_grad_all = jnp.concatenate([key_grad_all, value_grad_all], axis=1)
-    owned_out, kv_grad = fold(
-        out_term, kv_grad_all.astype(jnp.bfloat16).reshape(seq_count, rows, -1), seq_count, dp_count, 4
+    owned_out, kv_grad, got_early = fold(
+        out_term, kv_grad_all.astype(jnp.bfloat16).reshape(seq_count, rows, -1), passed, (0, 1), seq_count, dp_count, 4
     )
     key_rot_grad = kv_grad[:, :HEAD_DIM]
     value_grad = kv_grad[:, HEAD_DIM:]
@@ -1075,7 +975,12 @@
     qkv_term = jnp.where(
         jnp.arange(qkv_pad, dtype=jnp.int32)[None, :, None] == qkv_own, gain_rows[:, None, :], qkv_term
     )
-    owned_all, _ = fold(qkv_term, None, seq_count, dp_count, 5)
+    owned_all, _, got_late = fold(qkv_term, None, passed, (2,), seq_count, dp_count, 5)
+    grads_ffn = [kept[0], kept[1], kept[2]]
+    for i in range(groups // 2 - 1):
+        for m, piece in enumerate((got_early[i, 0], got_early[i, 1], got_late[i, 0])):
+            grads_ffn[m] = grads_ffn[m] + piece.astype(jnp.float32)
+    grad_w_gate, grad_w_up, grad_w_down = grads_ffn
     owned_qkv = owned_all[:qkv_own]
     owned = owned_all[qkv_own]
     own_width, own_head = width // count, HEAD_DIM // count

time: 388 us -> 359 us (0.925)
  Pallas kernels: 317 us -> 302 us
  starting transfers between devices: 5.79 us -> 0 us
    pallas_call x4, Pallas kernels: 164 us -> 145 us  [the longest x2 72.5 us: spread(): pl.pallas_call(functools.partial(spread_kernel, zs, ys, xs, kv is not Non...]
    ppermute x4 -> x0, starting transfers between devices: 5.79 us -> none  [swapped(): return lax.ppermute(value, axis, [(i, i ^ bit) for i in range(length)])]
  transfers between devices with their start and end apart: 4 -> 0, of which waited for: 0 -> 0; matrix products, arithmetic and copies ran while one was open for 7% -> 0% of each run, Pallas kernels for 34% -> 0%
where the time goes in v2:
time: 359 us
  Pallas kernels  302 us (84%)
  matrix products  22.7 us (6%)
  other arithmetic  21.9 us (6%)
  local copies, waits for them, and re-layouts  11.1 us (3%)
    pallas_call x1, Pallas kernels, ffn_block(): pl.pallas_call(functools.partial(ffn_kernel, zs, ys, ws, rows, width, own...  157 us
    pallas_call x2, Pallas kernels, spread(): pl.pallas_call(functools.partial(spread_kernel, zs, ys, xs, kv is not Non...  72.5 us
    pallas_call x2, Pallas kernels, fold(): pl.pallas_call(functools.partial(fold_kernel, zs, ys, xs, kv is not None,...  72.4 us
    dot_general x4, matrix products, contract_cols(): lax.dot_general(left, right, (((1,), (1,)), ((), ())), preferred_element_...  7.31 us

profile of v2, /device:TPU:0, one launch (start us, length us, event | category | flops | bytes accessed | tf_op | source)
XLA Modules:
  0.0 359.0 jit_solution(14223687182569079652)
XLA Ops:
  0.8 1.2 fusion.17
  2.0 0.5 copy-done.55
  2.6 2.5 fusion.7
  5.1 1.7 pad.9.refs_0_
  6.8 37.1 %spread.2 = (bf16[4,2,2,2,40,1536]{5,4,3,2,1,0:T(8,128)(2,1)}, bf16[1,216,1152]{2,1,0:T(8,128)(2,1)}, bf16[1,216,1152]{2,1,0:T(8,128)(2,1)}) custom-call(bf16[40,1536]{1,0:T(8,128)(2,1)} %pad.9.refs_0_, bf16[216,1152]{1,0:T(8,128)(2,1)} %refs_4_.1, bf16[216,1152]{1,0:T(8,128)(2,1)} %refs_5_.1), custom_call_target="tpu_custom_call" | custom-call | flops 1048576 | bytes 25165824 | tf_op jit(solution)/shard_map/spread/pallas_call | solution.py:646
  43.9 2.8 fusion.46
  47.0 0.2 reduce-window_clone.1
  47.4 0.5 fusion.41
  48.1 0.2 reshape.326
  48.3 0.2 multiply_reduce_fusion.11
  48.6 0.1 fusion.27
  48.8 0.9 fusion.23
  49.7 0.7 pad_maximum_fusion.5.refs_1_
  50.4 35.4 %spread.3 = (bf16[4,2,2,2,32,1152]{5,4,3,2,1,0:T(8,128)(2,1)}, bf16[4,128,512]{2,1,0:T(8,128)(2,1)}, bf16[1,216,1152]{2,1,0:T(8,128)(2,1)}) custom-call(bf16[32,1152]{1,0:T(8,128)(2,1)} %refs_0_.1, bf16[128,512]{1,0:T(8,128)(2,1)} %pad_maximum_fusion.5.refs_1_, bf16[216,1152]{1,0:T(8,128)(2,1)} %refs_6_.1), custom_call_target="tpu_custom_call" | custom-call | flops 1048576 | bytes 25165824 | tf_op jit(solution)/shard_map/spread/pallas_call | solution.py:646
  85.9 0.2 fusion.31
  86.1 0.4 copy-done.32
  86.5 1.7 select_reduce_fusion
  88.3 0.6 log_bitcast_fusion
  88.8 0.4 copy-done.58
  89.2 0.2 copy-done.53
  89.4 1.3 convolution_convert_fusion.3
  90.8 0.2 copy.82
  91.0 0.6 multiply_reduce_fusion.7
  91.6 0.3 multiply_reduce_fusion.6
  91.9 0.8 copy-done.2
  92.7 0.8 multiply_convert_fusion.1.refs_0_
  93.6 0.6 broadcast_in_dim.84.refs_3_
  94.2 156.7 %ffn_block.1 = (f32[128,1152]{1,0:T(8,128)}, f32[1,1152]{1,0:T(1,128)}, f32[128,1152]{1,0:T(8,128)}, f32[3,216,1152]{2,1,0:T(8,128)}, bf16[1,3,216,1152]{3,2,1,0:T(8,128)(2,1)}) custom-call(bf16[128,1152]{1,0:T(8,128)(2,1)} %multiply_convert_fusion.1.refs_0_, f32[128,1152]{1,0:T(8,128)} %copy-done.2, f32[128,1152]{1,0:T(8,128)} %bitcast.156, ...), custom_call_target="tpu_custom_call" | custom-call | flops 18345885696 | bytes 41943040 | tf_op jit(solution)/shard_map/ffn_block/pallas_call | solution.py:464
  250.9 1.7 multiply_reduce_fusion
  252.6 2.1 multiply_reduce_fusion.1
  254.7 0.2 multiply_convert_fusion
  255.0 0.9 convolution_convert_fusion.2
  255.9 0.2 copy.83
  256.1 0.1 copy.85
  256.2 0.1 multiply_reduce_fusion.10
  256.4 1.8 fusion.9
  258.2 0.3 fusion.11
  258.6 0.2 fusion.33
  258.8 0.5 fusion.12
  259.4 0.8 pad_maximum_fusion.refs_1_
  260.2 2.2 convolution_convert_fusion.1
  262.4 35.7 %fold.2 = (f32[32,1152]{1,0:T(8,128)}, f32[128,512]{1,0:T(8,128)}, bf16[1,2,216,1152]{3,2,1,0:T(8,128)(2,1)}) custom-call(bf16[4,2,2,2,32,1152]{5,4,3,2,1,0:T(8,128)(2,1)} %bitcast.148, bf16[4,128,512]{2,1,0:T(8,128)(2,1)} %pad_maximum_fusion.refs_1_, bf16[1,3,216,1152]{3,2,1,0:T(8,128)(2,1)} %get-tuple-element.37.refs_2_.refs_1_), custom_call_target="tpu_custom_call" | custom-call | flops 1048576 | bytes 25165824 | tf_op jit(solution)/shard_map/fold/pallas_call | solution.py:816
  298.2 1.4 broadcast_multiply_fusion.2
  299.6 0.3 broadcast_multiply_fusion
  300.0 0.3 multiply_reduce_fusion.8
  300.3 0.2 multiply_convert_fusion.3
  300.5 0.2 copy.86
  300.8 1.2 multiply_reduce_fusion.12
  302.0 1.0 multiply_convert_fusion.5
  303.3 3.6 fusion.37
  306.9 1.3 fusion
  308.3 1.5 multiply_reduce_fusion.2
  309.8 0.1 reshape.330
  310.1 0.1 reshape.331
  310.7 1.2 convolution_convert_fusion
  311.9 2.2 broadcast_select_fusion.refs_0_
  314.2 36.7 %fold.3 = (f32[40,1536]{1,0:T(8,128)}, bf16[1,1,216,1152]{3,2,1,0:T(8,128)(2,1)}) custom-call(bf16[4,2,2,2,40,1536]{5,4,3,2,1,0:T(8,128)(2,1)} %broadcast_select_fusion.refs_0_, bf16[1,3,216,1152]{3,2,1,0:T(8,128)(2,1)} %get-tuple-element.37.refs_2_.refs_1_), custom_call_target="tpu_custom_call" | custom-call | flops 1048576 | bytes 25165824 | tf_op jit(solution)/shard_map/fold/pallas_call | solution.py:816
  350.9 3.7 %convert_add_fusion.1 = (f32[216,1152]{1,0:T(8,128)}, f32[216,1152]{1,0:T(8,128)}, f32[216,1152]{1,0:T(8,128)}) fusion(f32[3,216,1152]{2,1,0:T(8,128)} %get-tuple-element.42, bf16[1,2,216,1152]{3,2,1,0:T(8,128)(2,1)S(1)} %copy-done.18, bf16[1,1,216,1152]{3,2,1,0:T(8,128)(2,1)} %get-tuple-element.44), kind=kLoop, calls=%fused_computation.30 | loop fusion | flops 1492992 | bytes 7464960 | tf_op jit(solution)/shard_map/add | solution.py:982
  354.6 0.6 slice_bitcast_fusion.6
  355.2 0.6 slice_bitcast_fusion.9
  355.8 1.0 add_bitcast_fusion
  356.8 0.8 copy.117
  357.6 0.7 copy.118
  358.3 0.7 copy.119
  (156 shorter events, 2.1 us)
Async XLA Ops:
  0.8 45.9 %copy-start.39 = (s32[1280]{0:T(1024)}, s32[1280]{0:T(1024)S(1)}, u32[]{:S(2)}) copy-start(s32[1280]{0:T(1024)S(1)} %select_n.46) | copy-start | bytes 15364
  2.0 0.5 copy-start.55
  5.0 42.9 %copy-start.10 = (bf16[128,1280]{1,0:T(8,128)(2,1)}, bf16[128,1280]{1,0:T(8,128)(2,1)S(1)}, u32[]{:S(2)}) copy-start(bf16[128,1280]{1,0:T(8,128)(2,1)S(1)} %fusion.7) | copy-start | bytes 983044
  5.0 41.8 %copy-start.34 = (f32[256]{0:T(256)S(1)}, f32[256]{0:T(256)}, u32[]{:S(2)}) copy-start(f32[256]{0:T(256)} %param.24) | copy-start | bytes 3076
  5.1 41.9 %copy-start.57 = (s32[1,4]{1,0:T(1,128)S(1)}, s32[1,4]{1,0:T(1,128)}, u32[]{:S(2)}) copy-start(s32[1,4]{1,0:T(1,128)} %param.16) | copy-start | bytes 52
  43.9 4.8 %copy-start.36 = (f32[256]{0:T(256)S(1)}, f32[256]{0:T(256)}, u32[]{:S(2)}) copy-start(f32[256]{0:T(256)} %param.23) | copy-start | bytes 3076
  46.7 3.0 copy-start.9
  46.9 1.2 copy-start.42
  47.0 38.9 %copy-start.48 = (s32[128]{0:T(128)}, s32[128]{0:T(128)S(1)}, u32[]{:S(2)}) copy-start(s32[128]{0:T(128)S(1)} %iota_add_fusion) | copy-start | bytes 1540
  47.3 38.6 %copy-start.50 = (s32[128]{0:T(128)}, s32[128]{0:T(128)S(1)}, u32[]{:S(2)}) copy-start(s32[128]{0:T(128)S(1)} %select_reduce_fusion.2) | copy-start | bytes 1540
  47.4 0.6 copy-start.16
  48.1 40.2 %copy-start = (f32[128,1024]{1,0:T(8,128)}, f32[128,1024]{1,0:T(8,128)S(1)}, u32[]{:S(2)}) copy-start(f32[128,1024]{1,0:T(8,128)S(1)} %slice.141) | copy-start | bytes 1572868
  48.6 1.8 copy-start.30
  85.8 5.2 %copy-start.5 = (bf16[4,2,2,2,32,1152]{5,4,3,2,1,0:T(8,128)(2,1)S(1)}, bf16[4,2,2,2,32,1152]{5,4,3,2,1,0:T(8,128)(2,1)}, u32[]{:S(2)}) copy-start(bf16[4,2,2,2,32,1152]{5,4,3,2,1,0:T(8,128)(2,1)} %get-tuple-element.31) | copy-start | bytes 7077892
  85.8 5.8 %copy-start.7 = (f32[1,128,1152]{2,1,0:T(8,128)S(1)}, f32[1,128,1152]{2,1,0:T(8,128)}, u32[]{:S(2)}) copy-start(f32[1,128,1152]{2,1,0:T(8,128)} %param.14) | copy-start | bytes 1769476
  85.8 5.8 %copy-start.26 = (f32[1152]{0:T(1024)S(1)}, f32[1152]{0:T(1024)}, u32[]{:S(2)}) copy-start(f32[1152]{0:T(1024)} %param.25) | copy-start | bytes 13828
  85.9 0.6 copy-start.32
  86.5 2.3 copy-start.28
  88.2 1.0 copy-start.58
  88.2 4.5 %copy-start.25 = (f32[1152]{0:T(1024)S(1)}, f32[1152]{0:T(1024)}, u32[]{:S(2)}) copy-start(f32[1152]{0:T(1024)} %param.26) | copy-start | bytes 13828
  88.8 0.6 copy-start.53
  89.4 4.1 %copy-start.41 = (f32[1152]{0:T(1024)S(1)}, f32[1152]{0:T(1024)}, u32[]{:S(2)}) copy-start(f32[1152]{0:T(1024)} %param.27) | copy-start | bytes 13828
  90.8 2.8 copy-start.14
  91.0 2.6 copy-start.12
  91.6 2.0 copy-start.3
  91.6 2.6 copy-start.44
  91.9 0.8 copy-start.2
  91.9 2.2 copy-start.46
  250.8 3.9 %copy-start.4 = (f32[128,1152]{1,0:T(8,128)S(1)}, f32[128,1152]{1,0:T(8,128)}, u32[]{:S(2)}) copy-start(f32[128,1152]{1,0:T(8,128)} %copy-done.3) | copy-start | bytes 1769476
  250.9 3.9 %copy-start.27 = (f32[1152]{0:T(1024)S(1)}, f32[1152]{0:T(1024)}, u32[]{:S(2)}) copy-start(f32[1152]{0:T(1024)} %param.25) | copy-start | bytes 13828
  250.9 3.9 %copy-start.45 = (f32[128]{0:T(128)S(1)}, f32[128]{0:T(128)}, u32[]{:S(2)}) copy-start(f32[128]{0:T(128)} %copy-done.44) | copy-start | bytes 1540
  250.9 4.0 %copy-start.6 = (bf16[4,2,2,2,32,1152]{5,4,3,2,1,0:T(8,128)(2,1)S(1)}, bf16[4,2,2,2,32,1152]{5,4,3,2,1,0:T(8,128)(2,1)}, u32[]{:S(2)}) copy-start(bf16[4,2,2,2,32,1152]{5,4,3,2,1,0:T(8,128)(2,1)} %get-tuple-element.31) | copy-start | bytes 7077892
  252.6 3.7 %copy-start.15 = (bf16[128,4,256]{2,0,1:T(8,128)(2,1)S(1)}, bf16[128,4,256]{2,0,1:T(8,128)(2,1)}, u32[]{:S(2)}) copy-start(bf16[128,4,256]{2,0,1:T(8,128)(2,1)} %copy-done.14) | copy-start | bytes 786436
  252.6 3.8 %copy-start.24 = (bf16[4,128,512]{2,1,0:T(8,128)(2,1)S(1)}, bf16[4,128,512]{2,1,0:T(8,128)(2,1)}, u32[]{:S(2)}) copy-start(bf16[4,128,512]{2,1,0:T(8,128)(2,1)} %get-tuple-element.30) | copy-start | bytes 1572868
  252.6 3.8 %copy-start.29 = (pred[128,512]{1,0:T(8,128)(4,1)S(1)}, pred[128,512]{1,0:T(8,128)(4,1)}, u32[]{:S(2)}) copy-start(pred[128,512]{1,0:T(8,128)(4,1)} %copy-done.28) | copy-start | bytes 196612
  252.6 3.8 %copy-start.54 = (f32[128,4]{0,1:T(4,128)S(1)}, f32[128,4]{0,1:T(4,128)}, u32[]{:S(2)}) copy-start(f32[128,4]{0,1:T(4,128)} %copy-done.53) | copy-start | bytes 6148
  254.7 3.5 copy-start.21
  254.9 3.7 %copy-start.33 = (s32[512]{0:T(512)S(1)}, s32[512]{0:T(512)}, u32[]{:S(2)}) copy-start(s32[512]{0:T(512)} %copy-done.32) | copy-start | bytes 6148
  254.9 3.7 %copy-start.49 = (s32[128]{0:T(128)S(1)}, s32[128]{0:T(128)}, u32[]{:S(2)}) copy-start(s32[128]{0:T(128)} %copy-done.48) | copy-start | bytes 1540
  255.0 3.7 %copy-start.51 = (s32[128]{0:T(128)S(1)}, s32[128]{0:T(128)}, u32[]{:S(2)}) copy-start(s32[128]{0:T(128)} %copy-done.50) | copy-start | bytes 1540
  255.0 3.8 %copy-start.52 = (f32[4,128]{1,0:T(4,128)S(1)}, f32[4,128]{1,0:T(4,128)}, u32[]{:S(2)}) copy-start(f32[4,128]{1,0:T(4,128)} %get-tuple-element.83) | copy-start | bytes 6148
  256.1 4.1 %copy-start.13 = (bf16[128,4,256]{0,2,1:T(8,128)(2,1)S(1)}, bf16[128,4,256]{0,2,1:T(8,128)(2,1)}, u32[]{:S(2)}) copy-start(bf16[128,4,256]{0,2,1:T(8,128)(2,1)} %copy-done.12) | copy-start | bytes 786436
  256.2 2.6 copy-start.59
  259.3 38.8 %copy-start.17 = (f32[128,128]{1,0:T(8,128)S(1)}, f32[128,128]{1,0:T(8,128)}, u32[]{:S(2)}) copy-start(f32[128,128]{1,0:T(8,128)} %copy-done.16) | copy-start | bytes 196612
  262.4 37.6 %copy-start.1 = (f32[128,1024]{1,0:T(8,128)S(1)}, f32[128,1024]{1,0:T(8,128)}, u32[]{:S(2)}) copy-start(f32[128,1024]{1,0:T(8,128)} %copy-done) | copy-start | bytes 1572868
  262.4 37.6 %copy-start.31 = (f32[128,4]{0,1:T(4,128)S(1)}, f32[128,4]{0,1:T(4,128)}, u32[]{:S(2)}) copy-start(f32[128,4]{0,1:T(4,128)} %copy-done.30) | copy-start | bytes 6148
  262.4 37.6 %copy-start.37 = (f32[256]{0:T(256)S(1)}, f32[256]{0:T(256)}, u32[]{:S(2)}) copy-start(f32[256]{0:T(256)} %param.23) | copy-start | bytes 3076
  298.2 2.6 copy-start.20
  298.2 2.6 copy-start.35
  298.2 2.5 copy-start.43
  300.3 6.6 %copy-start.40 = (s32[1280]{0:T(1024)S(1)}, s32[1280]{0:T(1024)}, u32[]{:S(2)}) copy-start(s32[1280]{0:T(1024)} %copy-done.39) | copy-start | bytes 15364
  303.3 5.0 %copy-start.8 = (f32[1,128,1152]{2,1,0:T(8,128)S(1)}, f32[1,128,1152]{2,1,0:T(8,128)}, u32[]{:S(2)}) copy-start(f32[1,128,1152]{2,1,0:T(8,128)} %param.14) | copy-start | bytes 1769476
  303.3 5.0 %copy-start.38 = (f32[1152]{0:T(1024)S(1)}, f32[1152]{0:T(1024)}, u32[]{:S(2)}) copy-start(f32[1152]{0:T(1024)} %param.22) | copy-start | bytes 13828
  303.3 5.0 %copy-start.56 = (f32[128]{0:T(128)S(1)}, f32[128]{0:T(128)}, u32[]{:S(2)}) copy-start(f32[128]{0:T(128)} %copy-done.55) | copy-start | bytes 1540
  306.9 3.5 copy-start.47
  306.9 3.8 %copy-start.11 = (bf16[128,1280]{1,0:T(8,128)(2,1)S(1)}, bf16[128,1280]{1,0:T(8,128)(2,1)}, u32[]{:S(2)}) copy-start(bf16[128,1280]{1,0:T(8,128)(2,1)} %copy-done.10) | copy-start | bytes 983044
  314.2 36.7 %copy-start.18 = (bf16[1,2,216,1152]{3,2,1,0:T(8,128)(2,1)S(1)}, bf16[1,2,216,1152]{3,2,1,0:T(8,128)(2,1)}, u32[]{:S(2)}) copy-start(bf16[1,2,216,1152]{3,2,1,0:T(8,128)(2,1)} %get-tuple-element.43) | copy-start | bytes 2985988
  350.9 3.7 %copy-start.22 = (f32[40,1536]{1,0:T(8,128)S(1)}, f32[40,1536]{1,0:T(8,128)}, u32[]{:S(2)}) copy-start(f32[40,1536]{1,0:T(8,128)} %get-tuple-element.40) | copy-start | bytes 737284
  350.9 5.9 %copy-start.19 = (f32[128,1152]{1,0:T(8,128)S(1)}, f32[128,1152]{1,0:T(8,128)}, u32[]{:S(2)}) copy-start(f32[128,1152]{1,0:T(8,128)} %get-tuple-element.35) | copy-start | bytes 1769476
  350.9 7.4 %copy-start.23 = (f32[32,1152]{1,0:T(8,128)S(1)}, f32[32,1152]{1,0:T(8,128)}, u32[]{:S(2)}) copy-start(f32[32,1152]{1,0:T(8,128)} %get-tuple-element.109) | copy-start | bytes 442372
